TPU v7x, 256 devices: a whole 4x4x8 slice. The times are simulated.
256 devices in a mesh: cuts: 8 (over x, y_lo), layer: 32 (over z, y_hi, core).
Axes of the slice: x: 4, y: 4 (y_hi: 2, y_lo: 2; y = y_hi * 2 + y_lo), z: 8, core: 2. Of those that a mesh axis runs over, the one named last changes fastest.
Arguments:
- vectors: float32 [8, 64, 64, 1024], P('cuts', None, 'layer'), may hold values from -40 to 40
- diag_blocks: bfloat16 [64, 1024, 1024], P('layer'), may hold values from -1 to 1, as said below
- couplings: bfloat16 [64, 1024, 1024], P('layer'), may hold values from -0.09375 to 0.09375
- bounds: int32 [8, 2], P('cuts'), may hold values from -128 to 160, as said below
Outputs:
- filtered: float32 [8, 64, 64, 1024], P('cuts', None, 'layer')
Inputs may be any that keep to these rules, and one draw needn't show every extreme that they name: `bounds`: column 0 holds each slice's lower end, which is -128 at slice 0 and to at most -81; column 1 holds its upper end, from 128 to 160. `diag_blocks`: each block is symmetric.
All inputs are finite; a program needn't handle non-finite values.
Results may differ from a plain program's by a relative error of at most 0.012.
Values may be sent and summed in bfloat16 or wider, within the bound.
A program may use at most 64 MiB of HBM per device.

v0:
```python
import jax
import jax.numpy as jnp
from jax import lax
from jax.sharding import PartitionSpec as P

EDGE = 16
DEG = 4


def shifted(block, axis, distance):
    devices = range(lax.axis_size(axis))
    route = [(i - distance, i) for i in devices if i - distance in devices]
    return lax.ppermute(block, axis, route)


def extended(block, sides, width):
    for axis, dim in sides:
        count = lax.axis_size(axis)
        forward = [(i, i + 1) for i in range(count - 1)]
        backward = [(target, source) for source, target in forward]
        low = lax.ppermute(
            lax.slice_in_dim(block, block.shape[dim] - width, None, axis=dim), axis, forward
        )
        high = lax.ppermute(lax.slice_in_dim(block, 0, width, axis=dim), axis, backward)
        block = jnp.concatenate([low, block, high], axis=dim)
    return block


def inner_products(first, second):
    return jnp.einsum("kn,jn->kj", first, second, precision=lax.Precision.HIGHEST)


def left_solve(factor, right_side):
    return lax.linalg.triangular_solve(factor, right_side, left_side=True, lower=True)


def per_device(vectors, diag_blocks, couplings, bounds):
    current_block = vectors[0]
    count_vec, layers, width = current_block.shape
    length_all = lax.axis_size("layer") * layers * width
    bottom = bounds[0, 0].astype(jnp.float32) / 64.0
    summit = bounds[0, 1].astype(jnp.float32) / 64.0
    centre = (bottom + summit) / 2.0
    half_width = (summit - bottom) / 2.0
    arrived_link = shifted(couplings[layers - 1 :], "layer", 1)
    links_below = jnp.concatenate([arrived_link, couplings[: layers - 1]], 0)

    def apply_operator(vectors_now):
        rounded = vectors_now.astype(jnp.bfloat16)
        padded = extended(rounded, (("layer", 1),), 1)
        result = jnp.einsum(
            "kld,lde->kle", rounded, diag_blocks, preferred_element_type=jnp.float32
        )
        result = result + jnp.einsum(
            "kle,lde->kld", padded[:, 2:], couplings, preferred_element_type=jnp.float32
        )
        return result + jnp.einsum(
            "kld,lde->kle", padded[:, :-2], links_below, preferred_element_type=jnp.float32
        )

    def filter_block(start):
        previous = start
        current = (apply_operator(start) - centre * start) / half_width
        for degree_index in range(DEG - 1):
            following = 2.0 * (apply_operator(current) - centre * current) / half_width - previous
            previous = current
            current = following
        return current

    def orthonormal(filtered):
        flat = filtered.reshape(count_vec, layers * width)
        gram = lax.psum(inner_products(flat, flat), "layer") / length_all
        return left_solve(jnp.linalg.cholesky(gram), flat)

    current_block = orthonormal(filter_block(current_block)).reshape(count_vec, layers, width)
    filtered = filter_block(current_block)
    final = orthonormal(filtered)
    low_edge = final[:EDGE]
    high_edge = final[count_vec - EDGE :]
    below_high = shifted(high_edge.astype(jnp.bfloat16), "cuts", 1).astype(high_edge.dtype)
    above_low = shifted(low_edge.astype(jnp.bfloat16), "cuts", -1).astype(low_edge.dtype)
    correlation_low, correlation_high = lax.psum(
        (inner_products(below_high, low_edge), inner_products(above_low, high_edge)), "layer"
    )
    low_new = low_edge - jnp.einsum(
        "wv,wn->vn", correlation_low / length_all, below_high, precision=lax.Precision.HIGHEST
    )
    high_new = high_edge - jnp.einsum(
        "wv,wn->vn", correlation_high / length_all, above_low, precision=lax.Precision.HIGHEST
    )
    result = jnp.concatenate([low_new, final[EDGE : count_vec - EDGE], high_new], 0)
    return result.reshape(1, count_vec, layers, width)


def solution(mesh):
    in_specs = (
        P("cuts", None, "layer", None),
        P("layer", None, None),
        P("layer", None, None),
        P("cuts", None),
    )
    out_specs = P("cuts", None, "layer", None)
    return jax.shard_map(
        per_device, mesh=mesh, in_specs=in_specs, out_specs=out_specs, check_vma=False
    )
```

profile of v0, /device:TPU:138, one launch (start us, length us, event | category | flops | bytes accessed | tf_op | source)
XLA Modules:
  0.0 574.1 jit_solution(272118990598733513)
XLA Ops:
  0.0 2.8 fusion.112
  2.9 2.2 collective-permute-start.1
  5.3 4.3 collective-permute-start.2
  9.6 4.9 collective-permute-start
  14.5 0.9 convolution_bitcast_fusion.8
  17.2 1.4 fusion.24
  18.6 17.0 %collective-permute-done.2 = bf16[64,1,1024]{2,0,1:T(8,128)(2,1)S(1)} collective-permute-done((bf16[64,1,1024]{2,0,1:T(8,128)(2,1)S(1)}, bf16[64,1,1024]{2,0,1:T(8,128)(2,1)S(1)}, u32[]{:S(2)}, u32[]{:S(2)}) %collective-permute-start.2) | collective-permute-done | bytes 131104 | tf_op jit(solution)/shard_map/ppermute | solution.py:21
  35.6 1.0 fusion.123
  36.7 4.5 collective-permute-start.4
  41.1 0.9 fusion.129
  42.0 4.7 collective-permute-start.3
  46.7 0.8 convolution_bitcast_fusion.6
  47.6 1.6 collective-permute-done.3
  49.2 1.6 fusion.124
  50.8 2.5 collective-permute-start.6
  53.3 0.9 fusion.130
  54.2 6.8 %collective-permute-start.5 = (bf16[64,1,1024]{2,0,1:T(8,128)(2,1)S(1)}, bf16[64,1,1024]{2,0,1:T(8,128)(2,1)S(1)}, u32[]{:S(2)}, u32[]{:S(2)}) collective-permute-start(bf16[64,1,1024]{2,0,1:T(8,128)(2,1)S(1)} %get-tuple-element.23), channel_id=1, source_target_pairs={{1,0},{2,1},{3,2},{4,3},{5,4},{6,5},{7,6},{8,7},{9,8},{10,9},{11,1... | collective-permute-start | bytes 393224 | tf_op jit(solution)/shard_map/ppermute | solution.py:24
  61.0 0.8 convolution_bitcast_fusion.5
  61.9 1.6 collective-permute-done.5
  63.5 1.5 fusion.125
  65.0 1.9 collective-permute-start.8
  67.0 0.9 fusion.131
  67.8 7.4 %collective-permute-start.7 = (bf16[64,1,1024]{2,0,1:T(8,128)(2,1)S(1)}, bf16[64,1,1024]{2,0,1:T(8,128)(2,1)S(1)}, u32[]{:S(2)}, u32[]{:S(2)}) collective-permute-start(bf16[64,1,1024]{2,0,1:T(8,128)(2,1)S(1)} %get-tuple-element.21), channel_id=1, source_target_pairs={{1,0},{2,1},{3,2},{4,3},{5,4},{6,5},{7,6},{8,7},{9,8},{10,9},{11,1... | collective-permute-start | bytes 393224 | tf_op jit(solution)/shard_map/ppermute | solution.py:24
  75.2 0.8 convolution_bitcast_fusion.4
  76.1 1.6 collective-permute-done.7
  77.7 1.5 fusion.41
  79.8 134.1 %psum.28 = f32[64,64]{0,1:T(8,128)S(1)} all-reduce(f32[64,64]{0,1:T(8,128)S(1)} %convolution_bitcast_fusion.11), channel_id=1, replica_groups=mesh['cuts'=8,'layer'=32] {'layer'}, use_global_device_ids=true, to_apply=%region_0.0 | all-reduce | flops 4096 | bytes 32768 | tf_op jit(solution)/shard_map/psum | solution.py:72
  214.0 5.8 %cholesky.44 = f32[64,64]{1,0:T(8,128)S(1)} custom-call(f32[64,64]{1,0:T(8,128)S(1)} %fusion.87), custom_call_target="Cholesky" | custom-call | tf_op jit(solution)/shard_map/jit(cholesky)/cholesky | solution.py:73
  219.9 0.7 compare_reduce_fusion.1
  221.2 4.9 custom-call.6
  226.9 1.9 collective-permute-start.10
  228.8 3.0 fusion.132
  231.9 7.5 %collective-permute-start.9 = (bf16[64,1,1024]{2,0,1:T(8,128)(2,1)S(1)}, bf16[64,1,1024]{2,0,1:T(8,128)(2,1)S(1)}, u32[]{:S(2)}, u32[]{:S(2)}) collective-permute-start(bf16[64,1,1024]{2,0,1:T(8,128)(2,1)S(1)} %get-tuple-element.19), channel_id=1, source_target_pairs={{1,0},{2,1},{3,2},{4,3},{5,4},{6,5},{7,6},{8,7},{9,8},{10,9},{11,1... | collective-permute-start | bytes 393224 | tf_op jit(solution)/shard_map/ppermute | solution.py:24
  239.4 0.8 convolution_bitcast_fusion.3
  240.3 1.6 collective-permute-done.9
  241.9 1.4 fusion.126
  243.3 1.9 collective-permute-start.12
  245.3 0.8 fusion.133
  246.1 7.4 %collective-permute-start.11 = (bf16[64,1,1024]{2,0,1:T(8,128)(2,1)S(1)}, bf16[64,1,1024]{2,0,1:T(8,128)(2,1)S(1)}, u32[]{:S(2)}, u32[]{:S(2)}) collective-permute-start(bf16[64,1,1024]{2,0,1:T(8,128)(2,1)S(1)} %get-tuple-element.17), channel_id=1, source_target_pairs={{1,0},{2,1},{3,2},{4,3},{5,4},{6,5},{7,6},{8,7},{9,8},{10,9},{11,1... | collective-permute-start | bytes 393224 | tf_op jit(solution)/shard_map/ppermute | solution.py:24
  253.5 0.8 convolution_bitcast_fusion.2
  254.4 1.6 collective-permute-done.11
  256.0 1.4 fusion.127
  257.5 1.9 collective-permute-start.14
  259.4 0.8 fusion.134
  260.3 7.4 %collective-permute-start.13 = (bf16[64,1,1024]{2,0,1:T(8,128)(2,1)S(1)}, bf16[64,1,1024]{2,0,1:T(8,128)(2,1)S(1)}, u32[]{:S(2)}, u32[]{:S(2)}) collective-permute-start(bf16[64,1,1024]{2,0,1:T(8,128)(2,1)S(1)} %get-tuple-element.15), channel_id=1, source_target_pairs={{1,0},{2,1},{3,2},{4,3},{5,4},{6,5},{7,6},{8,7},{9,8},{10,9},{11,1... | collective-permute-start | bytes 393224 | tf_op jit(solution)/shard_map/ppermute | solution.py:24
  267.7 0.8 convolution_bitcast_fusion.1
  268.5 1.6 collective-permute-done.13
  270.2 1.4 fusion.128
  271.6 1.9 collective-permute-start.16
  273.6 0.8 fusion.135
  274.4 7.6 %collective-permute-start.15 = (bf16[64,1,1024]{2,0,1:T(8,128)(2,1)S(1)}, bf16[64,1,1024]{2,0,1:T(8,128)(2,1)S(1)}, u32[]{:S(2)}, u32[]{:S(2)}) collective-permute-start(bf16[64,1,1024]{2,0,1:T(8,128)(2,1)S(1)} %get-tuple-element.13), channel_id=1, source_target_pairs={{1,0},{2,1},{3,2},{4,3},{5,4},{6,5},{7,6},{8,7},{9,8},{10,9},{11,1... | collective-permute-start | bytes 393224 | tf_op jit(solution)/shard_map/ppermute | solution.py:24
  282.0 0.8 convolution_bitcast_fusion
  282.9 1.4 collective-permute-done.15
  284.3 1.4 fusion.38
  286.3 134.0 %psum.29 = f32[64,64]{0,1:T(8,128)S(1)} all-reduce(f32[64,64]{0,1:T(8,128)S(1)} %convolution_bitcast_fusion.10), channel_id=1, replica_groups=mesh['cuts'=8,'layer'=32] {'layer'}, use_global_device_ids=true, to_apply=%region_3.6 | all-reduce | flops 4096 | bytes 32768 | tf_op jit(solution)/shard_map/psum | solution.py:72
  420.4 5.8 %cholesky.55 = f32[64,64]{1,0:T(8,128)S(1)} custom-call(f32[64,64]{1,0:T(8,128)S(1)} %fusion.84), custom_call_target="Cholesky" | custom-call | tf_op jit(solution)/shard_map/jit(cholesky)/cholesky | solution.py:73
  426.3 0.6 compare_reduce_fusion
  426.9 0.7 fusion.81
  427.6 4.9 custom-call.7
  433.2 3.3 collective-permute-start.17
  436.5 2.6 collective-permute-start.18
  439.6 4.0 collective-permute-done.18
  443.7 128.6 %all-reduce = (f32[16,16]{1,0:T(8,128)S(1)}, f32[16,16]{1,0:T(8,128)S(1)}) all-reduce(f32[16,16]{1,0:T(8,128)S(1)} %fusion.76, f32[16,16]{1,0:T(8,128)S(1)} %fusion.78), channel_id=1, replica_groups=mesh['cuts'=8,'layer'=32] {'layer'}, use_global_device_ids=true, to_apply=%region_5.8 | all-reduce | flops 512 | bytes 4096 | tf_op jit(solution)/shard_map/psum | solution.py:82
  572.9 1.2 reshape.38
  (59 shorter events, 5.6 us)
Async XLA Ops:
  0.0 5.1 copy-start.4
  0.0 14.4 %copy-start = (bf16[2,1024,1024]{2,1,0:T(8,128)(2,1)S(1)}, bf16[2,1024,1024]{2,1,0:T(8,128)(2,1)}, u32[]{:S(2)}) copy-start(bf16[2,1024,1024]{2,1,0:T(8,128)(2,1)} %param.8) | copy-start | bytes 12582916
  2.8 12.5 %copy-start.5 = (s32[1,2]{1,0:T(1,128)S(1)}, s32[1,2]{1,0:T(1,128)}, u32[]{:S(2)}) copy-start(s32[1,2]{1,0:T(1,128)} %param.10) | copy-start | bytes 28
  2.9 14.4 %copy-start.2 = (bf16[2,1024,1024]{2,1,0:T(8,128)(2,1)S(1)}, bf16[2,1024,1024]{2,1,0:T(8,128)(2,1)}, u32[]{:S(2)}) copy-start(bf16[2,1024,1024]{2,1,0:T(8,128)(2,1)} %param.9) | copy-start | bytes 12582916
  2.9 32.7 %collective-permute-start.1 = (bf16[1,1024,1024]{2,1,0:T(8,128)(2,1)S(1)}, bf16[1,1024,1024]{2,1,0:T(8,128)(2,1)S(1)}, u32[]{:S(2)}, u32[]{:S(2)}) collective-permute-start(bf16[1,1024,1024]{2,1,0:T(8,128)(2,1)S(1)} %get-tuple-element.9), channel_id=1, source_target_pairs={{0,1},{1,2},{2,3},{3,4},{4,5},{5,6},{6,7},{7,8},{8,9},{9,10},{10,1... | collective-permute-start | bytes 6291464 | tf_op jit(solution)/shard_map/ppermute | solution.py:13
  5.3 30.3 %collective-permute-start.2 = (bf16[64,1,1024]{2,0,1:T(8,128)(2,1)S(1)}, bf16[64,1,1024]{2,0,1:T(8,128)(2,1)S(1)}, u32[]{:S(2)}, u32[]{:S(2)}) collective-permute-start(bf16[64,1,1024]{2,0,1:T(8,128)(2,1)S(1)} %get-tuple-element.27), channel_id=1, source_target_pairs={{0,1},{1,2},{2,3},{3,4},{4,5},{5,6},{6,7},{7,8},{8,9},{9,10},{10,1... | collective-permute-start | bytes 393224 | tf_op jit(solution)/shard_map/ppermute | solution.py:21
  9.6 7.6 %collective-permute-start = (bf16[64,1,1024]{2,0,1:T(8,128)(2,1)S(1)}, bf16[64,1,1024]{2,0,1:T(8,128)(2,1)S(1)}, u32[]{:S(2)}, u32[]{:S(2)}) collective-permute-start(bf16[64,1,1024]{2,0,1:T(8,128)(2,1)S(1)} %get-tuple-element.28), channel_id=1, source_target_pairs={{1,0},{2,1},{3,2},{4,3},{5,4},{6,5},{7,6},{8,7},{9,8},{10,9},{11,1... | collective-permute-start | bytes 393224 | tf_op jit(solution)/shard_map/ppermute | solution.py:24
  35.6 39.6 %copy-start.6 = (bf16[1,1024,1024]{2,1,0:T(8,128)(2,1)}, bf16[1,1024,1024]{2,1,0:T(8,128)(2,1)S(1)}, u32[]{:S(2)}) copy-start(bf16[1,1024,1024]{2,1,0:T(8,128)(2,1)S(1)} %collective-permute-done.1) | copy-start | bytes 6291460
  36.7 10.1 %collective-permute-start.4 = (bf16[64,1,1024]{2,0,1:T(8,128)(2,1)S(1)}, bf16[64,1,1024]{2,0,1:T(8,128)(2,1)S(1)}, u32[]{:S(2)}, u32[]{:S(2)}) collective-permute-start(bf16[64,1,1024]{2,0,1:T(8,128)(2,1)S(1)} %get-tuple-element.26), channel_id=1, source_target_pairs={{0,1},{1,2},{2,3},{3,4},{4,5},{5,6},{6,7},{7,8},{8,9},{9,10},{10,1... | collective-permute-start | bytes 393224 | tf_op jit(solution)/shard_map/ppermute | solution.py:21
  42.0 7.2 %collective-permute-start.3 = (bf16[64,1,1024]{2,0,1:T(8,128)(2,1)S(1)}, bf16[64,1,1024]{2,0,1:T(8,128)(2,1)S(1)}, u32[]{:S(2)}, u32[]{:S(2)}) collective-permute-start(bf16[64,1,1024]{2,0,1:T(8,128)(2,1)S(1)} %get-tuple-element.25), channel_id=1, source_target_pairs={{1,0},{2,1},{3,2},{4,3},{5,4},{6,5},{7,6},{8,7},{9,8},{10,9},{11,1... | collective-permute-start | bytes 393224 | tf_op jit(solution)/shard_map/ppermute | solution.py:24
  50.8 10.2 %collective-permute-start.6 = (bf16[64,1,1024]{2,0,1:T(8,128)(2,1)S(1)}, bf16[64,1,1024]{2,0,1:T(8,128)(2,1)S(1)}, u32[]{:S(2)}, u32[]{:S(2)}) collective-permute-start(bf16[64,1,1024]{2,0,1:T(8,128)(2,1)S(1)} %get-tuple-element.24), channel_id=1, source_target_pairs={{0,1},{1,2},{2,3},{3,4},{4,5},{5,6},{6,7},{7,8},{8,9},{9,10},{10,1... | collective-permute-start | bytes 393224 | tf_op jit(solution)/shard_map/ppermute | solution.py:21
  54.2 9.3 %collective-permute-start.5 = (bf16[64,1,1024]{2,0,1:T(8,128)(2,1)S(1)}, bf16[64,1,1024]{2,0,1:T(8,128)(2,1)S(1)}, u32[]{:S(2)}, u32[]{:S(2)}) collective-permute-start(bf16[64,1,1024]{2,0,1:T(8,128)(2,1)S(1)} %get-tuple-element.23), channel_id=1, source_target_pairs={{1,0},{2,1},{3,2},{4,3},{5,4},{6,5},{7,6},{8,7},{9,8},{10,9},{11,1... | collective-permute-start | bytes 393224 | tf_op jit(solution)/shard_map/ppermute | solution.py:24
  65.0 10.2 %collective-permute-start.8 = (bf16[64,1,1024]{2,0,1:T(8,128)(2,1)S(1)}, bf16[64,1,1024]{2,0,1:T(8,128)(2,1)S(1)}, u32[]{:S(2)}, u32[]{:S(2)}) collective-permute-start(bf16[64,1,1024]{2,0,1:T(8,128)(2,1)S(1)} %get-tuple-element.22), channel_id=1, source_target_pairs={{0,1},{1,2},{2,3},{3,4},{4,5},{5,6},{6,7},{7,8},{8,9},{9,10},{10,1... | collective-permute-start | bytes 393224 | tf_op jit(solution)/shard_map/ppermute | solution.py:21
  67.8 9.9 %collective-permute-start.7 = (bf16[64,1,1024]{2,0,1:T(8,128)(2,1)S(1)}, bf16[64,1,1024]{2,0,1:T(8,128)(2,1)S(1)}, u32[]{:S(2)}, u32[]{:S(2)}) collective-permute-start(bf16[64,1,1024]{2,0,1:T(8,128)(2,1)S(1)} %get-tuple-element.21), channel_id=1, source_target_pairs={{1,0},{2,1},{3,2},{4,3},{5,4},{6,5},{7,6},{8,7},{9,8},{10,9},{11,1... | collective-permute-start | bytes 393224 | tf_op jit(solution)/shard_map/ppermute | solution.py:24
  226.2 13.2 %copy-start.7 = (bf16[1,1024,1024]{2,1,0:T(8,128)(2,1)S(1)}, bf16[1,1024,1024]{2,1,0:T(8,128)(2,1)}, u32[]{:S(2)}) copy-start(bf16[1,1024,1024]{2,1,0:T(8,128)(2,1)} %copy-done.6) | copy-start | bytes 6291460
  226.9 12.5 %collective-permute-start.10 = (bf16[64,1,1024]{2,0,1:T(8,128)(2,1)S(1)}, bf16[64,1,1024]{2,0,1:T(8,128)(2,1)S(1)}, u32[]{:S(2)}, u32[]{:S(2)}) collective-permute-start(bf16[64,1,1024]{2,0,1:T(8,128)(2,1)S(1)} %get-tuple-element.20), channel_id=1, source_target_pairs={{0,1},{1,2},{2,3},{3,4},{4,5},{5,6},{6,7},{7,8},{8,9},{9,10},{10,1... | collective-permute-start | bytes 393224 | tf_op jit(solution)/shard_map/ppermute | solution.py:21
  231.8 10.0 %copy-start.3 = (bf16[2,1024,1024]{2,1,0:T(8,128)(2,1)S(1)}, bf16[2,1024,1024]{2,1,0:T(8,128)(2,1)}, u32[]{:S(2)}) copy-start(bf16[2,1024,1024]{2,1,0:T(8,128)(2,1)} %param.9) | copy-start | bytes 12582916
  231.9 10.0 %collective-permute-start.9 = (bf16[64,1,1024]{2,0,1:T(8,128)(2,1)S(1)}, bf16[64,1,1024]{2,0,1:T(8,128)(2,1)S(1)}, u32[]{:S(2)}, u32[]{:S(2)}) collective-permute-start(bf16[64,1,1024]{2,0,1:T(8,128)(2,1)S(1)} %get-tuple-element.19), channel_id=1, source_target_pairs={{1,0},{2,1},{3,2},{4,3},{5,4},{6,5},{7,6},{8,7},{9,8},{10,9},{11,1... | collective-permute-start | bytes 393224 | tf_op jit(solution)/shard_map/ppermute | solution.py:24
  240.3 5.0 copy-start.1
  243.3 10.2 %collective-permute-start.12 = (bf16[64,1,1024]{2,0,1:T(8,128)(2,1)S(1)}, bf16[64,1,1024]{2,0,1:T(8,128)(2,1)S(1)}, u32[]{:S(2)}, u32[]{:S(2)}) collective-permute-start(bf16[64,1,1024]{2,0,1:T(8,128)(2,1)S(1)} %get-tuple-element.18), channel_id=1, source_target_pairs={{0,1},{1,2},{2,3},{3,4},{4,5},{5,6},{6,7},{7,8},{8,9},{9,10},{10,1... | collective-permute-start | bytes 393224 | tf_op jit(solution)/shard_map/ppermute | solution.py:21
  246.1 9.9 %collective-permute-start.11 = (bf16[64,1,1024]{2,0,1:T(8,128)(2,1)S(1)}, bf16[64,1,1024]{2,0,1:T(8,128)(2,1)S(1)}, u32[]{:S(2)}, u32[]{:S(2)}) collective-permute-start(bf16[64,1,1024]{2,0,1:T(8,128)(2,1)S(1)} %get-tuple-element.17), channel_id=1, source_target_pairs={{1,0},{2,1},{3,2},{4,3},{5,4},{6,5},{7,6},{8,7},{9,8},{10,9},{11,1... | collective-permute-start | bytes 393224 | tf_op jit(solution)/shard_map/ppermute | solution.py:24
  257.5 10.2 %collective-permute-start.14 = (bf16[64,1,1024]{2,0,1:T(8,128)(2,1)S(1)}, bf16[64,1,1024]{2,0,1:T(8,128)(2,1)S(1)}, u32[]{:S(2)}, u32[]{:S(2)}) collective-permute-start(bf16[64,1,1024]{2,0,1:T(8,128)(2,1)S(1)} %get-tuple-element.16), channel_id=1, source_target_pairs={{0,1},{1,2},{2,3},{3,4},{4,5},{5,6},{6,7},{7,8},{8,9},{9,10},{10,1... | collective-permute-start | bytes 393224 | tf_op jit(solution)/shard_map/ppermute | solution.py:21
  260.3 9.9 %collective-permute-start.13 = (bf16[64,1,1024]{2,0,1:T(8,128)(2,1)S(1)}, bf16[64,1,1024]{2,0,1:T(8,128)(2,1)S(1)}, u32[]{:S(2)}, u32[]{:S(2)}) collective-permute-start(bf16[64,1,1024]{2,0,1:T(8,128)(2,1)S(1)} %get-tuple-element.15), channel_id=1, source_target_pairs={{1,0},{2,1},{3,2},{4,3},{5,4},{6,5},{7,6},{8,7},{9,8},{10,9},{11,1... | collective-permute-start | bytes 393224 | tf_op jit(solution)/shard_map/ppermute | solution.py:24
  271.6 10.4 %collective-permute-start.16 = (bf16[64,1,1024]{2,0,1:T(8,128)(2,1)S(1)}, bf16[64,1,1024]{2,0,1:T(8,128)(2,1)S(1)}, u32[]{:S(2)}, u32[]{:S(2)}) collective-permute-start(bf16[64,1,1024]{2,0,1:T(8,128)(2,1)S(1)} %get-tuple-element.14), channel_id=1, source_target_pairs={{0,1},{1,2},{2,3},{3,4},{4,5},{5,6},{6,7},{7,8},{8,9},{9,10},{10,1... | collective-permute-start | bytes 393224 | tf_op jit(solution)/shard_map/ppermute | solution.py:21
  274.4 9.9 %collective-permute-start.15 = (bf16[64,1,1024]{2,0,1:T(8,128)(2,1)S(1)}, bf16[64,1,1024]{2,0,1:T(8,128)(2,1)S(1)}, u32[]{:S(2)}, u32[]{:S(2)}) collective-permute-start(bf16[64,1,1024]{2,0,1:T(8,128)(2,1)S(1)} %get-tuple-element.13), channel_id=1, source_target_pairs={{1,0},{2,1},{3,2},{4,3},{5,4},{6,5},{7,6},{8,7},{9,8},{10,9},{11,1... | collective-permute-start | bytes 393224 | tf_op jit(solution)/shard_map/ppermute | solution.py:24
  433.2 6.2 %collective-permute-start.17 = (bf16[16,2048]{1,0:T(8,128)(2,1)S(1)}, bf16[16,2048]{1,0:T(8,128)(2,1)S(1)}, u32[]{:S(2)}, u32[]{:S(2)}) collective-permute-start(bf16[16,2048]{1,0:T(8,128)(2,1)S(1)} %get-tuple-element.11), channel_id=1, source_target_pairs={{0,32},{32,64},{64,96},{96,128},{128,160},{160,192},{192,224},{1,3... | collective-permute-start | bytes 196616 | tf_op jit(solution)/shard_map/ppermute | solution.py:13
  436.5 7.1 %collective-permute-start.18 = (bf16[16,2048]{1,0:T(8,128)(2,1)S(1)}, bf16[16,2048]{1,0:T(8,128)(2,1)S(1)}, u32[]{:S(2)}, u32[]{:S(2)}) collective-permute-start(bf16[16,2048]{1,0:T(8,128)(2,1)S(1)} %get-tuple-element.12), channel_id=1, source_target_pairs={{32,0},{64,32},{96,64},{128,96},{160,128},{192,160},{224,192},{33,... | collective-permute-start | bytes 196616 | tf_op jit(solution)/shard_map/ppermute | solution.py:13
where the time goes:
time: 575 us; the launch traced here: 574 us
  blocking collectives  397 us (69%)
  starting transfers between devices  82.6 us (14%)
  waiting for transfers between devices  32.6 us (6%)
  matrix products  30.7 us (5%)
  other arithmetic  24.2 us (4%)
    psum x2, blocking collectives, orthonormal(): gram = lax.psum(inner_products(flat, flat), 'layer') / length_all  268 us
    psum x1, blocking collectives, per_device(): lax.psum((inner_products(below_high, low_edge), inner_products(above_low,...  129 us
    ppermute x8, starting transfers between devices, extended(): lax.ppermute(lax.slice_in_dim(block, 0, width, axis=dim), axis, backward)  53.7 us
    ppermute x8, starting transfers between devices, extended(): lax.ppermute(lax.slice_in_dim(block, block.shape[dim] - width, None, axis...  20.9 us
    ppermute x8, waiting for transfers between devices, extended(): lax.ppermute(lax.slice_in_dim(block, block.shape[dim] - width, None, axis...  17 us
    another operation x6, other arithmetic, orthonormal(): return left_solve(jnp.linalg.cholesky(gram), flat)  13.1 us
    dot_general x8, matrix products, apply_operator(): jnp.einsum('kle,lde->kld', padded[:, 2:], couplings, preferred_element_ty...  11.6 us
  transfers between devices with their start and end apart: 19, of which 10 were waited for; matrix products, arithmetic and copies ran while one was open for 3% of the time, Pallas kernels for 0%

commit v1 on v0

v1 whole, which is shorter than its diff:
```python
import functools

import jax
import jax.numpy as jnp
from jax import lax
from jax.experimental import pallas as pl
from jax.experimental.pallas import tpu as pltpu
from jax.sharding import PartitionSpec as P

EDGE = 16
DEG = 4
STEPS = 2
GROUP = 4
F32 = jnp.float32
BF16 = jnp.bfloat16
NN = (((1,), (0,)), ((), ()))
NT = (((1,), (1,)), ((), ()))
TN = (((0,), (0,)), ((), ()))
MESH = pl.DeviceIdType.MESH


def mm(a, b, dims=NN):
    return lax.dot_general(a, b, dims, preferred_element_type=F32)


def split(value):
    high = value.astype(BF16)
    return high, (value - high.astype(F32)).astype(BF16)


def cholesky_inverse(gram):
    n = gram.shape[0]
    rows = lax.broadcasted_iota(jnp.int32, (n, n), 0)
    lanes = lax.broadcasted_iota(jnp.int32, (n, n), 1)
    eye = (rows == lanes).astype(F32)
    whole = jnp.concatenate([gram, eye], axis=1)
    blocks = [whole[8 * b : 8 * b + 8] for b in range(n // 8)]
    inner = lax.broadcasted_iota(jnp.int32, (8, 2 * n), 0)
    for j in range(n):
        home = j // 8
        row = jnp.broadcast_to(blocks[home][j % 8 : j % 8 + 1], (8, 2 * n))
        pivot = jnp.broadcast_to(row[:, j : j + 1], (8, 2 * n))
        scaled = row / pivot
        for b in range(home, n // 8):
            column = jnp.broadcast_to(blocks[b][:, j : j + 1], (8, 2 * n))
            if b == home:
                column = jnp.where(inner > j % 8, column, 0.0)
            blocks[b] = blocks[b] - column * scaled
    whole = jnp.concatenate(blocks, axis=0)
    diagonal = jnp.sum(whole[:, :n] * eye, axis=1, keepdims=True)
    return whole[:, n:] * lax.rsqrt(diagonal)


def kernel(
    sizes, bounds, x_in, d_hbm, c_hbm, out,
    dv, cv, zf, zb, pb, rz, rp, acc, own, first, second, edge_out, edge_in,
    load_sem, zs, zr, ps, pr, a1s, a1r, a2s, a2r, es, er,
):
    n_cuts, n_layer = sizes
    n_z = n_layer // GROUP
    me = lax.axis_index("layer")
    cut = lax.axis_index("cuts")
    plane, member = me // GROUP, me % GROUP
    k, width = x_in.shape[1:]
    half = width // 2
    length_all = n_layer * 2 * width
    has_prev, has_next = me > 0, me < n_layer - 1
    has_below, has_above = cut > 0, cut < n_cuts - 1
    group_peer = [plane * GROUP + (member + q) % GROUP for q in range(1, GROUP)]
    plane_peer = [((plane + q) % n_z) * GROUP + member for q in range(1, n_z)]

    loads = []
    for i, (src, dst) in enumerate(((c_hbm, cv), (d_hbm, dv))):
        for l in (1, 0):
            loads.append(pltpu.make_async_copy(src.at[l], dst.at[l], load_sem.at[2 * i + l]))
    for copy in loads:
        copy.start()

    barrier = pltpu.get_barrier_semaphore()

    def greet(condition, device):
        @pl.when(condition)
        def _():
            pl.semaphore_signal(barrier, inc=1, device_id=device, device_id_type=MESH)

    for peer in group_peer + plane_peer:
        pl.semaphore_signal(barrier, inc=1, device_id={"layer": peer}, device_id_type=MESH)
    greet(has_prev, {"layer": me - 1})
    greet(has_next, {"layer": me + 1})
    greet(has_below, {"cuts": cut - 1})
    greet(has_above, {"cuts": cut + 1})

    low = bounds[0, 0].astype(F32) / 64.0
    high = bounds[0, 1].astype(F32) / 64.0
    centre = jnp.full((8, 128), (low + high) / 2.0, F32)[:1, :1]
    inverse = 1.0 / jnp.full((8, 128), (high - low) / 2.0, F32)[:1, :1]

    for l in range(2):
        zf[0, l] = x_in[l]
        zf[1, l] = jnp.zeros((k, width), F32)
        zb[0, l] = x_in[l].astype(BF16)

    @pl.when(jnp.logical_not(has_next))
    def _():
        rz[...] = jnp.zeros_like(rz)

    @pl.when(jnp.logical_not(has_prev))
    def _():
        rp[...] = jnp.zeros_like(rp)

    @pl.when(jnp.logical_not(has_below))
    def _():
        edge_in[0] = jnp.zeros_like(edge_in[0])

    @pl.when(jnp.logical_not(has_above))
    def _():
        edge_in[1] = jnp.zeros_like(edge_in[1])

    signals = (GROUP - 1) + (n_z - 1)
    for condition in (has_prev, has_next, has_below, has_above):
        signals = signals + jnp.where(condition, 1, 0)
    pl.semaphore_wait(barrier, signals)
    for copy in loads:
        copy.wait()

    def z_copy(t):
        return pltpu.make_async_remote_copy(
            zb.at[t, 0], rz.at[t], zs.at[t], zr.at[t],
            device_id={"layer": me - 1}, device_id_type=MESH,
        )

    def p_copy(t):
        return pltpu.make_async_remote_copy(
            pb.at[t], rp.at[t], ps.at[t], pr.at[t],
            device_id={"layer": me + 1}, device_id_type=MESH,
        )

    columns = [pl.ds(h * half, half) for h in range(2)]

    def apply_step(t, factor, back):
        cur, nxt = t % 2, (t + 1) % 2

        @pl.when(has_prev)
        def _():
            z_copy(t).start()

        for s in columns:
            pb[t, :, s] = mm(zb[t, 1], cv[1, :, s]).astype(BF16)

        @pl.when(has_next)
        def _():
            p_copy(t).start()

        for s in columns:
            acc[0, :, s] = mm(zb[t, 0], dv[0, :, s]) + mm(zb[t, 1], cv[0, s, :], NT)
            acc[1, :, s] = mm(zb[t, 1], dv[1, :, s]) + mm(zb[t, 0], cv[0, :, s])

        def update(l, s, total):
            now = zf[cur, l, :, s]
            value = (factor * inverse) * (total - centre * now) - back * zf[nxt, l, :, s]
            zf[nxt, l, :, s] = value
            zb[t + 1, l, :, s] = value.astype(BF16)

        @pl.when(has_next)
        def _():
            z_copy(t).wait_recv()

        for s in columns:
            update(1, s, acc[1, :, s] + mm(rz[t], cv[1, s, :], NT))

        @pl.when(has_prev)
        def _():
            p_copy(t).wait_recv()

        for s in columns:
            update(0, s, acc[0, :, s] + rp[t, :, s].astype(F32))

    def all_reduce(i, value):
        own[i, 0] = value
        sends = []
        for q, peer in enumerate(group_peer):
            sends.append(pltpu.make_async_remote_copy(
                own.at[i, 0], first.at[i, q], a1s.at[i, q], a1r.at[i, q],
                device_id={"layer": peer}, device_id_type=MESH,
            ))
        for copy in sends:
            copy.start()
        for copy in sends:
            copy.wait_recv()
        total = value
        for q in range(GROUP - 1):
            total = total + first[i, q]
        own[i, 1] = total
        more = []
        for q, peer in enumerate(plane_peer):
            more.append(pltpu.make_async_remote_copy(
                own.at[i, 1], second.at[i, q], a2s.at[i, q], a2r.at[i, q],
                device_id={"layer": peer}, device_id_type=MESH,
            ))
        for copy in more:
            copy.start()
        for copy in more:
            copy.wait_recv()
        for q in range(n_z - 1):
            total = total + second[i, q]
        for copy in sends + more:
            copy.wait_send()
        return total

    def orthonormal(i, src, store):
        gram = jnp.zeros((2 * k, 2 * k), F32)
        for l in range(2):
            pair = jnp.concatenate(split(zf[src, l]), axis=0)
            gram = gram + mm(pair, pair, NT)
        gram = gram[:k, :k] + gram[:k, k:] + gram[k:, :k]
        packed = jnp.concatenate([gram[: k // 2], gram[k // 2 :]], axis=1)
        packed = all_reduce(i, packed)
        gram = jnp.concatenate([packed[:, :k], packed[:, k:]], axis=0) * (1.0 / length_all)
        factor_high, factor_low = split(cholesky_inverse(gram))
        factors = jnp.concatenate([factor_high, factor_high, factor_low], axis=1)
        for l in range(2):
            y_high, y_low = split(zf[src, l])
            store(l, mm(factors, jnp.concatenate([y_high, y_low, y_high], axis=0)))

    def factor_of(t):
        return jnp.where(t == 0, 1.0, 2.0), jnp.where(t == 0, 0.0, 1.0)

    def first_filter(t, carry):
        apply_step(t, *factor_of(t))
        return carry

    def second_filter(t, carry):
        apply_step(t + DEG, *factor_of(t))
        return carry

    lax.fori_loop(0, DEG, first_filter, 0)

    def store_first(l, value):
        zf[0, l] = value
        zf[1, l] = jnp.zeros((k, width), F32)
        zb[DEG, l] = value.astype(BF16)

    orthonormal(0, 0, store_first)
    lax.fori_loop(0, DEG, second_filter, 0)

    def store_last(l, value):
        out[l] = value
        edge_out[0, l] = value[k - EDGE :].astype(BF16)
        edge_out[1, l] = value[:EDGE].astype(BF16)

    orthonormal(1, 0, store_last)

    to_above = pltpu.make_async_remote_copy(
        edge_out.at[0], edge_in.at[0], es.at[0], er.at[0],
        device_id={"cuts": cut + 1}, device_id_type=MESH,
    )
    to_below = pltpu.make_async_remote_copy(
        edge_out.at[1], edge_in.at[1], es.at[1], er.at[1],
        device_id={"cuts": cut - 1}, device_id_type=MESH,
    )
    pl.when(has_above)(to_above.start)
    pl.when(has_below)(to_below.start)
    pl.when(has_below)(to_above.wait_recv)
    pl.when(has_above)(to_below.wait_recv)

    edges = (slice(0, EDGE), slice(k - EDGE, k))
    parts = []
    for side in range(2):
        part = jnp.zeros((EDGE, EDGE), F32)
        for l in range(2):
            e_high, e_low = split(out[l, edges[side], :])
            other = edge_in[side, l]
            part = part + mm(other, e_high, NT) + mm(other, e_low, NT)
        parts.append(part)
    filler = jnp.zeros((EDGE, 128 - 2 * EDGE), F32)
    sums = jnp.concatenate(parts + [filler], axis=1)
    own_rows = own.shape[2]
    sums = jnp.concatenate([sums, jnp.zeros((own_rows - EDGE, 128), F32)], axis=0)
    sums = all_reduce(2, sums) * (1.0 / length_all)
    for side in range(2):
        c_high, c_low = split(sums[:EDGE, side * EDGE : (side + 1) * EDGE])
        for l in range(2):
            other = edge_in[side, l]
            out[l, edges[side], :] = (
                out[l, edges[side], :] - mm(c_high, other, TN) - mm(c_low, other, TN)
            )

    pl.when(has_above)(to_above.wait_send)
    pl.when(has_below)(to_below.wait_send)

    def drain(t, carry):
        pl.when(has_prev)(z_copy(t).wait_send)
        pl.when(has_next)(p_copy(t).wait_send)
        return carry

    lax.fori_loop(0, STEPS * DEG, drain, 0)


def per_device(sizes, vectors, diag_blocks, couplings, bounds):
    x = jnp.transpose(vectors[0], (1, 0, 2))
    _, k, width = x.shape
    n_z = sizes[1] // GROUP
    runs = STEPS * DEG
    vmem = pl.BlockSpec(memory_space=pltpu.VMEM)
    anywhere = pl.BlockSpec(memory_space=pl.ANY)
    dma = pltpu.SemaphoreType.DMA
    result = pl.pallas_call(
        functools.partial(kernel, sizes),
        out_shape=jax.ShapeDtypeStruct(x.shape, F32),
        in_specs=[pl.BlockSpec(memory_space=pltpu.SMEM), vmem, anywhere, anywhere],
        out_specs=vmem,
        scratch_shapes=[
            pltpu.VMEM((2, width, width), BF16),
            pltpu.VMEM((2, width, width), BF16),
            pltpu.VMEM((2, 2, k, width), F32),
            pltpu.VMEM((runs + 1, 2, k, width), BF16),
            pltpu.VMEM((runs, k, width), BF16),
            pltpu.VMEM((runs, k, width), BF16),
            pltpu.VMEM((runs, k, width), BF16),
            pltpu.VMEM((2, k, width), F32),
            pltpu.VMEM((3, 2, k // 2, 128), F32),
            pltpu.VMEM((3, GROUP - 1, k // 2, 128), F32),
            pltpu.VMEM((3, n_z - 1, k // 2, 128), F32),
            pltpu.VMEM((2, 2, EDGE, width), BF16),
            pltpu.VMEM((2, 2, EDGE, width), BF16),
            dma((4,)),
            dma((runs,)),
            dma((runs,)),
            dma((runs,)),
            dma((runs,)),
            dma((3, GROUP - 1)),
            dma((3, GROUP - 1)),
            dma((3, n_z - 1)),
            dma((3, n_z - 1)),
            dma((2,)),
            dma((2,)),
        ],
        compiler_params=pltpu.CompilerParams(
            collective_id=0, has_side_effects=True, vmem_limit_bytes=48 << 20
        ),
    )(bounds, x, diag_blocks, couplings)
    return jnp.transpose(result, (1, 0, 2))[None]


def solution(mesh):
    sizes = (mesh.shape["cuts"], mesh.shape["layer"])
    in_specs = (
        P("cuts", None, "layer", None),
        P("layer", None, None),
        P("layer", None, None),
        P("cuts", None),
    )
    return jax.shard_map(
        functools.partial(per_device, sizes),
        mesh=mesh,
        in_specs=in_specs,
        out_specs=P("cuts", None, "layer", None),
        check_vma=False,
    )
```

time: 575 us -> 115 us (0.20)
  the two profiles are of different devices: /device:TPU:138 before, /device:TPU:6 now
where the time goes in v1:
time: 115 us; the launch traced here: 114 us
  Pallas kernels  109 us (95%)
  local copies, waits for them, and re-layouts  5.25 us (5%)
    pallas_call x1, Pallas kernels, per_device(): pl.pallas_call(functools.partial(kernel, sizes), out_shape=jax.ShapeDtype...  109 us
    unnamed x5, local copies, waits for them, and re-layouts  4.05 us

profile of v1, /device:TPU:6, one launch (start us, length us, event | category | flops | bytes accessed | tf_op | source)
XLA Modules:
  0.0 114.4 jit_solution(8912951812438389139)
XLA Ops:
  0.0 1.2 %copy.8 = f32[1,64,2,1024]{3,1,2,0:T(8,128)S(1)} copy(f32[1,64,2,1024]{3,2,1,0:T(2,128)} %param.4) | data formatting | bytes 1048576 | tf_op args[0]
  1.2 0.0 copy-start
  1.2 2.2 %copy-done = bf16[2,1024,1024]{2,1,0:T(8,128)(2,1)S(1)} copy-done((bf16[2,1024,1024]{2,1,0:T(8,128)(2,1)S(1)}, bf16[2,1024,1024]{2,1,0:T(8,128)(2,1)}, u32[]{:S(2)}) %copy-start) | copy-done | bytes 4194328
  3.4 0.0 copy-start.1
  3.4 0.7 copy-done.1
  4.1 109.1 %shard_map.46 = f32[2,64,1024]{2,1,0:T(8,128)S(1)} custom-call(s32[1,2]{1,0:T(1,128)S(1)} %copy-done.1, f32[2,64,1024]{2,1,0:T(8,128)S(1)} %bitcast.9, bf16[2,1024,1024]{2,1,0:T(8,128)(2,1)S(1)} %copy-done, bf16[2,1024,1024]{2,1,0:T(8,128)(2,1)} %c_hbm.1), custom_call_target="tpu_custom_call" | custom-call | tf_op jit(solution)/shard_map/pallas_call | solution.py:307
  113.2 1.2 %copy.6 = f32[1,64,2,1024]{3,2,1,0:T(2,128)} copy(f32[1,64,2,1024]{3,1,2,0:T(8,128)S(1)} %bitcast.8) | data formatting | bytes 1048576 | tf_op jit(solution)/shard_map/broadcast_in_dim | solution.py:342
Async XLA Ops:
  1.2 2.2 %copy-start = (bf16[2,1024,1024]{2,1,0:T(8,128)(2,1)S(1)}, bf16[2,1024,1024]{2,1,0:T(8,128)(2,1)}, u32[]{:S(2)}) copy-start(bf16[2,1024,1024]{2,1,0:T(8,128)(2,1)} %d_hbm.1) | copy-start | bytes 12582916
  3.4 0.7 copy-start.1

commit v2 on v1

v2 whole, which is shorter than its diff:
```python
import functools

import jax
import jax.numpy as jnp
from jax import lax
from jax.experimental import pallas as pl
from jax.experimental.pallas import tpu as pltpu
from jax.sharding import PartitionSpec as P

EDGE = 16
DEG = 4
STEPS = 2
GROUP = 4
F32 = jnp.float32
BF16 = jnp.bfloat16
NN = (((1,), (0,)), ((), ()))
NT = (((1,), (1,)), ((), ()))
TN = (((0,), (0,)), ((), ()))
MESH = pl.DeviceIdType.MESH


def mm(a, b, dims=NN):
    return lax.dot_general(a, b, dims, preferred_element_type=F32)


def split(value):
    high = value.astype(BF16)
    return high, (value - high.astype(F32)).astype(BF16)


def cholesky_inverse(gram, group=4):
    n = gram.shape[0]
    rows_at = lax.broadcasted_iota(jnp.int32, (n, n), 0)
    lanes_at = lax.broadcasted_iota(jnp.int32, (n, n), 1)
    eye = (rows_at == lanes_at).astype(F32)
    whole = jnp.concatenate([gram, eye], axis=1)
    shape = (8, 2 * n)
    blocks = [whole[8 * b : 8 * b + 8] for b in range(n // 8)]
    inner = lax.broadcasted_iota(jnp.int32, shape, 0)
    for j in range(0, n, group):
        home, at = j // 8, j % 8
        active = range(home, n // 8)
        rows = [jnp.broadcast_to(blocks[home][at + i : at + i + 1], shape) for i in range(group)]
        cross = {
            (i, m): jnp.broadcast_to(rows[i][:, j + m : j + m + 1], shape)
            for i in range(group)
            for m in range(i, group)
        }
        columns = {
            (b, i): jnp.broadcast_to(blocks[b][:, j + i : j + i + 1], shape)
            for b in active
            for i in range(group)
        }
        for i in range(group):
            inverse = 1.0 / cross[i, i]
            scaled = rows[i] * inverse
            later = range(i + 1, group)
            ratio = {m: cross[i, m] * inverse for m in later}
            for m in later:
                rows[m] = rows[m] - cross[i, m] * scaled
                for q in range(m, group):
                    cross[m, q] = cross[m, q] - cross[i, m] * ratio[q]
            for b in active:
                column = columns[b, i]
                for m in later:
                    columns[b, m] = columns[b, m] - column * ratio[m]
                if b == home:
                    column = jnp.where(inner > at + i, column, 0.0)
                blocks[b] = blocks[b] - column * scaled
    whole = jnp.concatenate(blocks, axis=0)
    diagonal = jnp.sum(whole[:, :n] * eye, axis=1, keepdims=True)
    return whole[:, n:] * lax.rsqrt(diagonal)


def stacked_factor(factor):
    high, low = split(factor)
    return jnp.concatenate([high, high, low], axis=1)


def stacked_rows(rows):
    high, low = split(rows)
    return jnp.concatenate([high, low, high], axis=0)


def exact(a, b, dims):
    return lax.dot_general(
        a, b, dims, precision=lax.Precision.HIGHEST, preferred_element_type=F32
    )


def kernel(
    sizes, bounds_hbm, x_in, d_hbm, c_hbm, out,
    bounds, dv, cv, ct, zf, zb, pb, rz, rp, acc, own, first, second, factors,
    ylow_out, ylow_in, high_out, high_in, corr_out, corr_in,
    load_sem, zs, zr, ps, pr, a1s, a1r, a2s, a2r, es, er,
):
    n_cuts, n_layer = sizes
    n_z = n_layer // GROUP
    me = lax.axis_index("layer")
    cut = lax.axis_index("cuts")
    plane, member = me // GROUP, me % GROUP
    k, width = x_in.shape[1:]
    half = width // 2
    scale = 1.0 / (n_layer * 2 * width)
    has_prev, has_next = me > 0, me < n_layer - 1
    has_below, has_above = cut > 0, cut < n_cuts - 1
    group_peer = [plane * GROUP + (member + q) % GROUP for q in range(1, GROUP)]
    plane_peer = [((plane + q) % n_z) * GROUP + member for q in range(1, n_z)]

    bounds_load = pltpu.make_async_copy(bounds_hbm, bounds, load_sem.at[4])
    bounds_load.start()
    loads = []
    for i, (src, dst) in enumerate(((c_hbm, cv), (d_hbm, dv))):
        for l in (1, 0):
            loads.append(pltpu.make_async_copy(src.at[l], dst.at[l], load_sem.at[2 * i + l]))
    for copy in loads:
        copy.start()

    barrier = pltpu.get_barrier_semaphore()

    def greet(condition, device):
        @pl.when(condition)
        def _():
            pl.semaphore_signal(barrier, inc=1, device_id=device, device_id_type=MESH)

    for peer in plane_peer + group_peer:
        pl.semaphore_signal(barrier, inc=1, device_id={"layer": peer}, device_id_type=MESH)
    greet(has_prev, {"layer": me - 1})
    greet(has_next, {"layer": me + 1})
    greet(has_below, {"cuts": cut - 1})
    greet(has_above, {"cuts": cut + 1})

    for l in range(2):
        zf[0, l] = x_in[l]
        zf[1, l] = jnp.zeros((k, width), F32)
        zb[0, l] = x_in[l].astype(BF16)

    @pl.when(jnp.logical_not(has_next))
    def _():
        rz[...] = jnp.zeros_like(rz)

    @pl.when(jnp.logical_not(has_prev))
    def _():
        rp[...] = jnp.zeros_like(rp)

    @pl.when(jnp.logical_not(has_below))
    def _():
        high_in[...] = jnp.zeros_like(high_in)
        corr_in[...] = jnp.zeros_like(corr_in)

    @pl.when(jnp.logical_not(has_above))
    def _():
        ylow_in[...] = jnp.zeros_like(ylow_in)

    bounds_load.wait()
    low = bounds[0, 0].astype(F32) / 64.0
    high = bounds[0, 1].astype(F32) / 64.0
    centre = jnp.full((8, 128), (low + high) / 2.0, F32)[:1, :1]
    inverse = 1.0 / jnp.full((8, 128), (high - low) / 2.0, F32)[:1, :1]
    for copy in loads:
        copy.wait()
    for l in (1, 0):
        ct[l] = jnp.transpose(cv[l])

    signals = (GROUP - 1) + (n_z - 1)
    for condition in (has_prev, has_next, has_below, has_above):
        signals = signals + jnp.where(condition, 1, 0)
    pl.semaphore_wait(barrier, signals)

    columns = [pl.ds(h * half, half) for h in range(2)]

    def remote(src, dst, send, recv, device):
        return pltpu.make_async_remote_copy(
            src, dst, send, recv, device_id=device, device_id_type=MESH
        )

    def z_copy(t, h):
        return remote(
            zb.at[t, 0, :, columns[h]], rz.at[t, :, columns[h]], zs.at[t, h], zr.at[t, h],
            {"layer": me - 1},
        )

    def p_copy(t, h):
        return remote(
            pb.at[t, h], rp.at[t, h], ps.at[t, h], pr.at[t, h], {"layer": me + 1}
        )

    def group_copy(i, q):
        return remote(
            own.at[i, 0], first.at[i, q], a1s.at[i, q], a1r.at[i, q], {"layer": group_peer[q]}
        )

    def plane_copy(i, q):
        return remote(
            own.at[i, 1], second.at[i, q], a2s.at[i, q], a2r.at[i, q], {"layer": plane_peer[q]}
        )

    def reduce_start(i, value):
        own[i, 0] = value
        for q in range(GROUP - 1):
            group_copy(i, q).start()

    def reduce_middle(i):
        for q in range(GROUP - 1):
            group_copy(i, q).wait_recv()
        total = own[i, 0]
        for q in range(GROUP - 1):
            total = total + first[i, q]
        own[i, 1] = total
        for q in range(n_z - 1):
            plane_copy(i, q).start()

    def reduce_end(i):
        for q in range(n_z - 1):
            plane_copy(i, q).wait_recv()
        total = own[i, 1]
        for q in range(n_z - 1):
            total = total + second[i, q]
        return total

    def gram_start(i, src):
        gram = jnp.zeros((2 * k, 2 * k), F32)
        for l in range(2):
            pair = jnp.concatenate(split(zf[src, l]), axis=0)
            gram = gram + mm(pair, pair, NT)
        gram = gram[:k, :k] + gram[:k, k:] + gram[k:, :k]
        reduce_start(i, jnp.concatenate([gram[: k // 2], gram[k // 2 :]], axis=1))

    def gram_end(i):
        packed = reduce_end(i)
        return jnp.concatenate([packed[:, :k], packed[:, k:]], axis=0) * scale

    def apply_step(t, carry):
        cur, nxt = t % 2, (t + 1) % 2
        opening = t % DEG == 0
        factor, back = jnp.where(opening, 1.0, 2.0), jnp.where(opening, 0.0, 1.0)

        @pl.when(has_prev)
        def _():
            z_copy(t, 0).start()
            z_copy(t, 1).start()

        for h, s in enumerate(columns):
            pb[t, h] = mm(zb[t, 1], cv[1, :, s]).astype(BF16)

            @pl.when(has_next)
            def _():
                p_copy(t, h).start()

        pl.when(t == DEG)(lambda: gram_start(0, 0))

        acc[0] = mm(zb[t, 0], dv[0]) + mm(zb[t, 1], ct[0])
        acc[1] = mm(zb[t, 1], dv[1]) + mm(zb[t, 0], cv[0])

        pl.when(t == DEG)(lambda: reduce_middle(0))

        @pl.when(t == DEG + 1)
        def _():
            factors[0] = stacked_factor(cholesky_inverse(gram_end(0)))

        def update(l, s, total):
            now = zf[cur, l, :, s]
            value = (factor * inverse) * (total - centre * now) - back * zf[nxt, l, :, s]
            zf[nxt, l, :, s] = value
            zb[t + 1, l, :, s] = value.astype(BF16)

        pl.when(has_next)(lambda: z_copy(t, 0).wait_recv())
        acc[1] += mm(rz[t, :, columns[0]], ct[1, columns[0], :])
        pl.when(has_next)(lambda: z_copy(t, 1).wait_recv())
        everything = pl.ds(0, width)
        update(1, everything, acc[1] + mm(rz[t, :, columns[1]], ct[1, columns[1], :]))

        for h, s in enumerate(columns):
            pl.when(has_prev)(lambda: p_copy(t, h).wait_recv())
            update(0, s, acc[0, :, s] + rp[t, h].astype(F32))
        return carry

    runs = STEPS * DEG
    lax.fori_loop(0, runs, apply_step, 0)

    for l in range(2):
        value = mm(factors[0], stacked_rows(zf[0, l]))
        zf[0, l] = value
        ylow_out[l] = value[:EDGE].astype(BF16)

    below, above = {"cuts": cut - 1}, {"cuts": cut + 1}
    ylow_copy = remote(ylow_out, ylow_in, es.at[0], er.at[0], below)
    high_copy = remote(high_out, high_in, es.at[1], er.at[1], above)
    corr_copy = remote(corr_out, corr_in, es.at[2], er.at[2], above)
    pl.when(has_below)(ylow_copy.start)
    gram_start(1, 0)
    reduce_middle(1)

    pl.when(has_above)(ylow_copy.wait_recv)
    cross = jnp.zeros((k, EDGE), F32)
    corner = jnp.zeros((EDGE, EDGE), F32)
    for l in range(2):
        y_high, y_low = split(zf[0, l])
        cross = cross + mm(y_high, ylow_in[l], NT) + mm(y_low, ylow_in[l], NT)
        corner = corner + mm(ylow_in[l], ylow_in[l], NT)
    pieces = [cross[EDGE * i : EDGE * (i + 1)] for i in range(k // EDGE)] + [corner]
    pieces.append(jnp.zeros((EDGE, 128 - EDGE * len(pieces)), F32))
    packed = jnp.concatenate(pieces, axis=1)
    reduce_start(2, jnp.concatenate([packed, jnp.zeros((k // 2 - EDGE, 128), F32)], axis=0))
    reduce_middle(2)

    factor = cholesky_inverse(gram_end(1))
    factors[0] = stacked_factor(factor)
    factor_edge = factor[k - EDGE :]
    edge_rows = stacked_factor(factor_edge)
    for l in range(2):
        high_out[l] = mm(edge_rows, stacked_rows(zf[0, l])).astype(BF16)
    pl.when(has_above)(high_copy.start)
    for l in range(2):
        out[l] = mm(factors[0], stacked_rows(zf[0, l]))

    packed = reduce_end(2)[:EDGE] * scale
    cross = jnp.concatenate(
        [packed[:, EDGE * i : EDGE * (i + 1)] for i in range(k // EDGE)], axis=0
    )
    corner = packed[:, k : k + EDGE]
    rows_at = lax.broadcasted_iota(jnp.int32, (EDGE, EDGE), 0)
    lanes_at = lax.broadcasted_iota(jnp.int32, (EDGE, EDGE), 1)
    corner = jnp.where(has_above, corner, (rows_at == lanes_at).astype(F32))
    above_factor = cholesky_inverse(corner)
    corr = exact(exact(above_factor, cross, NT), factor_edge, NT)
    corr_out[...] = jnp.concatenate([corr, jnp.zeros((EDGE, 128 - EDGE), F32)], axis=1)
    pl.when(has_above)(corr_copy.start)

    f_high, f_low = split(above_factor)
    c_high, c_low = split(corr)
    for l in range(2):
        rows = mm(f_high, ylow_in[l]) + mm(f_low, ylow_in[l])
        r_high, r_low = split(rows)
        change = mm(c_high, r_high, TN) + mm(c_high, r_low, TN) + mm(c_low, r_high, TN)
        out[l, k - EDGE :, :] = out[l, k - EDGE :, :] - change

    pl.when(has_below)(high_copy.wait_recv)
    pl.when(has_below)(corr_copy.wait_recv)
    c_high, c_low = split(corr_in[:, :EDGE])
    for l in range(2):
        change = mm(c_high, high_in[l]) + mm(c_low, high_in[l])
        out[l, :EDGE, :] = out[l, :EDGE, :] - change

    pl.when(has_below)(ylow_copy.wait_send)
    pl.when(has_above)(high_copy.wait_send)
    pl.when(has_above)(corr_copy.wait_send)
    for i in range(3):
        for q in range(GROUP - 1):
            group_copy(i, q).wait_send()
        for q in range(n_z - 1):
            plane_copy(i, q).wait_send()

    def drain(t, carry):
        for h in range(2):
            pl.when(has_prev)(lambda: z_copy(t, h).wait_send())
            pl.when(has_next)(lambda: p_copy(t, h).wait_send())
        return carry

    lax.fori_loop(0, runs, drain, 0)


def per_device(sizes, vectors, diag_blocks, couplings, bounds):
    x = jnp.transpose(vectors[0], (1, 0, 2))
    _, k, width = x.shape
    n_z = sizes[1] // GROUP
    runs = STEPS * DEG
    vmem = pl.BlockSpec(memory_space=pltpu.VMEM)
    hbm = pl.BlockSpec(memory_space=pltpu.HBM)
    dma = pltpu.SemaphoreType.DMA
    result = pl.pallas_call(
        functools.partial(kernel, sizes),
        out_shape=jax.ShapeDtypeStruct(x.shape, F32),
        in_specs=[hbm, vmem, hbm, hbm],
        out_specs=vmem,
        scratch_shapes=[
            pltpu.SMEM((1, 2), jnp.int32),
            pltpu.VMEM((2, width, width), BF16),
            pltpu.VMEM((2, width, width), BF16),
            pltpu.VMEM((2, width, width), BF16),
            pltpu.VMEM((2, 2, k, width), F32),
            pltpu.VMEM((runs + 1, 2, k, width), BF16),
            pltpu.VMEM((runs, 2, k, width // 2), BF16),
            pltpu.VMEM((runs, k, width), BF16),
            pltpu.VMEM((runs, 2, k, width // 2), BF16),
            pltpu.VMEM((2, k, width), F32),
            pltpu.VMEM((3, 2, k // 2, 128), F32),
            pltpu.VMEM((3, GROUP - 1, k // 2, 128), F32),
            pltpu.VMEM((3, n_z - 1, k // 2, 128), F32),
            pltpu.VMEM((1, k, 3 * k), BF16),
            pltpu.VMEM((2, EDGE, width), BF16),
            pltpu.VMEM((2, EDGE, width), BF16),
            pltpu.VMEM((2, EDGE, width), BF16),
            pltpu.VMEM((2, EDGE, width), BF16),
            pltpu.VMEM((EDGE, 128), F32),
            pltpu.VMEM((EDGE, 128), F32),
            dma((5,)),
            dma((runs, 2)),
            dma((runs, 2)),
            dma((runs, 2)),
            dma((runs, 2)),
            dma((3, GROUP - 1)),
            dma((3, GROUP - 1)),
            dma((3, n_z - 1)),
            dma((3, n_z - 1)),
            dma((3,)),
            dma((3,)),
        ],
        compiler_params=pltpu.CompilerParams(
            collective_id=0, has_side_effects=True, vmem_limit_bytes=62 << 20
        ),
    )(bounds, x, diag_blocks, couplings)
    return jnp.transpose(result, (1, 0, 2))[None]


def solution(mesh):
    sizes = (mesh.shape["cuts"], mesh.shape["layer"])
    in_specs = (
        P("cuts", None, "layer", None),
        P("layer", None, None),
        P("layer", None, None),
        P("cuts", None),
    )
    return jax.shard_map(
        functools.partial(per_device, sizes),
        mesh=mesh,
        in_specs=in_specs,
        out_specs=P("cuts", None, "layer", None),
        check_vma=False,
    )
```

time: 115 us -> 84.6 us (0.74)
  Pallas kernels: 109 us -> 80 us
    pallas_call x1, Pallas kernels: 109 us -> 80 us  [per_device(): pl.pallas_call(functools.partial(kernel, sizes), out_shape=jax.ShapeDtype...]
    unnamed x5 -> x1, local copies, waits for them, and re-layouts: 4.05 us -> 2 us
where the time goes in v2:
time: 84.6 us; the launch traced here: 84.2 us
  Pallas kernels  80 us (95%)
  local copies, waits for them, and re-layouts  4.24 us (5%)
    pallas_call x1, Pallas kernels, per_device(): pl.pallas_call(functools.partial(kernel, sizes), out_shape=jax.ShapeDtype...  80 us
    broadcast_in_dim x1, local copies, waits for them, and re-layouts, per_device(): return jnp.transpose(result, (1, 0, 2))[None]  2.24 us
    unnamed x1, local copies, waits for them, and re-layouts  2 us

profile of v2, /device:TPU:6, one launch (start us, length us, event | category | flops | bytes accessed | tf_op | source)
XLA Modules:
  0.0 84.2 jit_solution(17789217961377295395)
XLA Ops:
  0.0 2.0 %copy.8 = f32[1,64,2,1024]{3,1,2,0:T(8,128)} copy(f32[1,64,2,1024]{3,2,1,0:T(2,128)} %param.4) | data formatting | bytes 1048576 | tf_op args[0]
  2.0 80.0 %shard_map.46 = f32[2,64,1024]{2,1,0:T(8,128)} custom-call(s32[1,2]{1,0:T(1,128)} %bounds_hbm.1, f32[2,64,1024]{2,1,0:T(8,128)} %bitcast.9, bf16[2,1024,1024]{2,1,0:T(8,128)(2,1)} %d_hbm.1, bf16[2,1024,1024]{2,1,0:T(8,128)(2,1)} %c_hbm.1), custom_call_target="tpu_custom_call" | custom-call | tf_op jit(solution)/shard_map/pallas_call | solution.py:371
  82.0 2.2 %copy.6 = f32[1,64,2,1024]{3,2,1,0:T(2,128)} copy(f32[1,64,2,1024]{3,1,2,0:T(8,128)} %bitcast.8) | data formatting | bytes 1048576 | tf_op jit(solution)/shard_map/broadcast_in_dim | solution.py:413

commit v3 on v2

--- a/solution.py
+++ b/solution.py
@@ -28,7 +28,7 @@
     return high, (value - high.astype(F32)).astype(BF16)
 
 
-def cholesky_inverse(gram, group=4):
+def cholesky_inverse(gram, group=8):
     n = gram.shape[0]
     rows_at = lax.broadcasted_iota(jnp.int32, (n, n), 0)
     lanes_at = lax.broadcasted_iota(jnp.int32, (n, n), 1)
@@ -90,23 +90,26 @@
 
 def kernel(
     sizes, bounds_hbm, x_in, d_hbm, c_hbm, out,
-    bounds, dv, cv, ct, zf, zb, pb, rz, rp, acc, own, first, second, factors,
+    bounds, x_own, dv, cv, ct, zf, zb, pb, rz, rp, acc, own, first, second, factors,
     ylow_out, ylow_in, high_out, high_in, corr_out, corr_in,
-    load_sem, zs, zr, ps, pr, a1s, a1r, a2s, a2r, es, er,
+    load_sem, zs, zr, ps, pr, a1s, a1r, a2s, a2r, es, er, ready,
 ):
     n_cuts, n_layer = sizes
     n_z = n_layer // GROUP
     me = lax.axis_index("layer")
     cut = lax.axis_index("cuts")
     plane, member = me // GROUP, me % GROUP
-    k, width = x_in.shape[1:]
+    k, _, width = x_in.shape
     half = width // 2
     scale = 1.0 / (n_layer * 2 * width)
     has_prev, has_next = me > 0, me < n_layer - 1
     has_below, has_above = cut > 0, cut < n_cuts - 1
     group_peer = [plane * GROUP + (member + q) % GROUP for q in range(1, GROUP)]
-    plane_peer = [((plane + q) % n_z) * GROUP + member for q in range(1, n_z)]
-
+    far_first = sorted(range(1, n_z), key=lambda q: -min(q, n_z - q))
+    plane_peer = [((plane + q) % n_z) * GROUP + member for q in far_first]
+
+    x_load = pltpu.make_async_copy(x_in, x_own, load_sem.at[5])
+    x_load.start()
     bounds_load = pltpu.make_async_copy(bounds_hbm, bounds, load_sem.at[4])
     bounds_load.start()
     loads = []
@@ -118,22 +121,19 @@
 
     barrier = pltpu.get_barrier_semaphore()
 
-    def greet(condition, device):
-        @pl.when(condition)
-        def _():
-            pl.semaphore_signal(barrier, inc=1, device_id=device, device_id_type=MESH)
-
-    for peer in plane_peer + group_peer:
-        pl.semaphore_signal(barrier, inc=1, device_id={"layer": peer}, device_id_type=MESH)
-    greet(has_prev, {"layer": me - 1})
-    greet(has_next, {"layer": me + 1})
-    greet(has_below, {"cuts": cut - 1})
-    greet(has_above, {"cuts": cut + 1})
-
-    for l in range(2):
-        zf[0, l] = x_in[l]
+    def ring(step):
+        return {"layer": (me + step + n_layer) % n_layer}
+
+    def greet(device):
+        pl.semaphore_signal(barrier, inc=1, device_id=device, device_id_type=MESH)
+
+    greet(ring(1))
+    greet(ring(-1))
+    pl.when(has_below)(lambda: greet({"cuts": cut - 1}))
+    pl.when(has_above)(lambda: greet({"cuts": cut + 1}))
+
+    for l in range(2):
         zf[1, l] = jnp.zeros((k, width), F32)
-        zb[0, l] = x_in[l].astype(BF16)
 
     @pl.when(jnp.logical_not(has_next))
     def _():
@@ -157,15 +157,25 @@
     high = bounds[0, 1].astype(F32) / 64.0
     centre = jnp.full((8, 128), (low + high) / 2.0, F32)[:1, :1]
     inverse = 1.0 / jnp.full((8, 128), (high - low) / 2.0, F32)[:1, :1]
-    for copy in loads:
-        copy.wait()
-    for l in (1, 0):
-        ct[l] = jnp.transpose(cv[l])
-
-    signals = (GROUP - 1) + (n_z - 1)
-    for condition in (has_prev, has_next, has_below, has_above):
-        signals = signals + jnp.where(condition, 1, 0)
-    pl.semaphore_wait(barrier, signals)
+    x_load.wait()
+    for l in range(2):
+        mine = x_own[:, l, :]
+        zf[0, l] = mine
+        zb[0, l] = mine.astype(BF16)
+
+    greeted = 2 + jnp.where(has_below, 1, 0) + jnp.where(has_above, 1, 0)
+    pl.semaphore_wait(barrier, greeted)
+
+    rounds = ready.shape[0]
+
+    def tell(r):
+        for step in (1 << r, -(1 << r)):
+            pl.semaphore_signal(
+                ready.at[r], inc=1, device_id=ring(step), device_id_type=MESH
+            )
+
+    def hear(r):
+        pl.semaphore_wait(ready.at[r], 2)
 
     columns = [pl.ds(h * half, half) for h in range(2)]
 
@@ -185,37 +195,41 @@
             pb.at[t, h], rp.at[t, h], ps.at[t, h], pr.at[t, h], {"layer": me + 1}
         )
 
+    lengths = [pl.ds(0, rows) for rows in (k // 2, k // 2, EDGE)]
+
     def group_copy(i, q):
         return remote(
-            own.at[i, 0], first.at[i, q], a1s.at[i, q], a1r.at[i, q], {"layer": group_peer[q]}
+            own.at[i, 0, lengths[i]], first.at[i, q, lengths[i]],
+            a1s.at[i, q], a1r.at[i, q], {"layer": group_peer[q]},
         )
 
     def plane_copy(i, q):
         return remote(
-            own.at[i, 1], second.at[i, q], a2s.at[i, q], a2r.at[i, q], {"layer": plane_peer[q]}
+            own.at[i, 1, lengths[i]], second.at[i, q, lengths[i]],
+            a2s.at[i, q], a2r.at[i, q], {"layer": plane_peer[q]},
         )
 
     def reduce_start(i, value):
-        own[i, 0] = value
+        own[i, 0, lengths[i]] = value
         for q in range(GROUP - 1):
             group_copy(i, q).start()
 
     def reduce_middle(i):
         for q in range(GROUP - 1):
             group_copy(i, q).wait_recv()
-        total = own[i, 0]
+        total = own[i, 0, lengths[i]]
         for q in range(GROUP - 1):
-            total = total + first[i, q]
-        own[i, 1] = total
+            total = total + first[i, q, lengths[i]]
+        own[i, 1, lengths[i]] = total
         for q in range(n_z - 1):
             plane_copy(i, q).start()
 
     def reduce_end(i):
         for q in range(n_z - 1):
             plane_copy(i, q).wait_recv()
-        total = own[i, 1]
+        total = own[i, 1, lengths[i]]
         for q in range(n_z - 1):
-            total = total + second[i, q]
+            total = total + second[i, q, lengths[i]]
         return total
 
     def gram_start(i, src):
@@ -240,6 +254,19 @@
             z_copy(t, 0).start()
             z_copy(t, 1).start()
 
+        @pl.when(t == 0)
+        def _():
+            tell(0)
+            loads[0].wait()
+
+        for r in range(rounds):
+
+            @pl.when(t == r + 1)
+            def _():
+                hear(r)
+                if r + 1 < rounds:
+                    tell(r + 1)
+
         for h, s in enumerate(columns):
             pb[t, h] = mm(zb[t, 1], cv[1, :, s]).astype(BF16)
 
@@ -247,14 +274,20 @@
             def _():
                 p_copy(t, h).start()
 
+        @pl.when(t == 0)
+        def _():
+            for copy in loads[1:]:
+                copy.wait()
+            for l in (1, 0):
+                ct[l] = jnp.transpose(cv[l])
+
         pl.when(t == DEG)(lambda: gram_start(0, 0))
+        pl.when(t == DEG + 1)(lambda: reduce_middle(0))
 
         acc[0] = mm(zb[t, 0], dv[0]) + mm(zb[t, 1], ct[0])
         acc[1] = mm(zb[t, 1], dv[1]) + mm(zb[t, 0], cv[0])
 
-        pl.when(t == DEG)(lambda: reduce_middle(0))
-
-        @pl.when(t == DEG + 1)
+        @pl.when(t == 2 * DEG - 1)
         def _():
             factors[0] = stacked_factor(cholesky_inverse(gram_end(0)))
 
@@ -301,7 +334,7 @@
     pieces = [cross[EDGE * i : EDGE * (i + 1)] for i in range(k // EDGE)] + [corner]
     pieces.append(jnp.zeros((EDGE, 128 - EDGE * len(pieces)), F32))
     packed = jnp.concatenate(pieces, axis=1)
-    reduce_start(2, jnp.concatenate([packed, jnp.zeros((k // 2 - EDGE, 128), F32)], axis=0))
+    reduce_start(2, packed)
     reduce_middle(2)
 
     factor = cholesky_inverse(gram_end(1))
@@ -312,9 +345,10 @@
         high_out[l] = mm(edge_rows, stacked_rows(zf[0, l])).astype(BF16)
     pl.when(has_above)(high_copy.start)
     for l in range(2):
-        out[l] = mm(factors[0], stacked_rows(zf[0, l]))
-
-    packed = reduce_end(2)[:EDGE] * scale
+        zf[1, l] = mm(factors[0], stacked_rows(zf[0, l]))
+        out[EDGE : k - EDGE, l, :] = zf[1, l, EDGE : k - EDGE]
+
+    packed = reduce_end(2) * scale
     cross = jnp.concatenate(
         [packed[:, EDGE * i : EDGE * (i + 1)] for i in range(k // EDGE)], axis=0
     )
@@ -333,14 +367,14 @@
         rows = mm(f_high, ylow_in[l]) + mm(f_low, ylow_in[l])
         r_high, r_low = split(rows)
         change = mm(c_high, r_high, TN) + mm(c_high, r_low, TN) + mm(c_low, r_high, TN)
-        out[l, k - EDGE :, :] = out[l, k - EDGE :, :] - change
+        out[k - EDGE :, l, :] = zf[1, l, k - EDGE :] - change
 
     pl.when(has_below)(high_copy.wait_recv)
     pl.when(has_below)(corr_copy.wait_recv)
     c_high, c_low = split(corr_in[:, :EDGE])
     for l in range(2):
         change = mm(c_high, high_in[l]) + mm(c_low, high_in[l])
-        out[l, :EDGE, :] = out[l, :EDGE, :] - change
+        out[:EDGE, l, :] = zf[1, l, :EDGE] - change
 
     pl.when(has_below)(ylow_copy.wait_send)
     pl.when(has_above)(high_copy.wait_send)
@@ -361,20 +395,22 @@
 
 
 def per_device(sizes, vectors, diag_blocks, couplings, bounds):
-    x = jnp.transpose(vectors[0], (1, 0, 2))
-    _, k, width = x.shape
+    x = vectors[0]
+    k, _, width = x.shape
     n_z = sizes[1] // GROUP
     runs = STEPS * DEG
+    rounds = (sizes[1] // 2).bit_length() - 1
     vmem = pl.BlockSpec(memory_space=pltpu.VMEM)
     hbm = pl.BlockSpec(memory_space=pltpu.HBM)
     dma = pltpu.SemaphoreType.DMA
     result = pl.pallas_call(
         functools.partial(kernel, sizes),
         out_shape=jax.ShapeDtypeStruct(x.shape, F32),
-        in_specs=[hbm, vmem, hbm, hbm],
+        in_specs=[hbm] * 4,
         out_specs=vmem,
         scratch_shapes=[
             pltpu.SMEM((1, 2), jnp.int32),
+            pltpu.VMEM((k, 2, width), F32),
             pltpu.VMEM((2, width, width), BF16),
             pltpu.VMEM((2, width, width), BF16),
             pltpu.VMEM((2, width, width), BF16),
@@ -394,7 +430,7 @@
             pltpu.VMEM((2, EDGE, width), BF16),
             pltpu.VMEM((EDGE, 128), F32),
             pltpu.VMEM((EDGE, 128), F32),
-            dma((5,)),
+            dma((6,)),
             dma((runs, 2)),
             dma((runs, 2)),
             dma((runs, 2)),
@@ -405,12 +441,13 @@
             dma((3, n_z - 1)),
             dma((3,)),
             dma((3,)),
+            pltpu.SemaphoreType.REGULAR((rounds,)),
         ],
         compiler_params=pltpu.CompilerParams(
-            collective_id=0, has_side_effects=True, vmem_limit_bytes=62 << 20
+            collective_id=0, has_side_effects=True, vmem_limit_bytes=61 << 20
         ),
     )(bounds, x, diag_blocks, couplings)
-    return jnp.transpose(result, (1, 0, 2))[None]
+    return result[None]
 
 
 def solution(mesh):

time: 84.6 us -> 75.4 us (0.89)
  Pallas kernels: 80 us -> 73.4 us
  local copies, waits for them, and re-layouts: 4.24 us -> 1.87 us
    pallas_call x1, Pallas kernels: 80 us -> 73.4 us  [per_device(): pl.pallas_call(functools.partial(kernel, sizes), out_shape=jax.ShapeDtype...]
    broadcast_in_dim x1 -> x0, local copies, waits for them, and re-layouts: 2.24 us -> none  [per_device(): return jnp.transpose(result, (1, 0, 2))[None]]
where the time goes in v3:
time: 75.4 us; the launch traced here: 75.3 us
  Pallas kernels  73.4 us (97%)
  local copies, waits for them, and re-layouts  1.87 us (2%)
    pallas_call x1, Pallas kernels, per_device(): pl.pallas_call(functools.partial(kernel, sizes), out_shape=jax.ShapeDtype...  73.4 us
    unnamed x1, local copies, waits for them, and re-layouts  1.87 us

profile of v3, /device:TPU:6, one launch (start us, length us, event | category | flops | bytes accessed | tf_op | source)
XLA Modules:
  0.0 75.3 jit_solution(17942756914625468821)
XLA Ops:
  0.0 73.4 %shard_map.46 = f32[64,2,1024]{2,1,0:T(2,128)} custom-call(s32[1,2]{1,0:T(1,128)} %bounds_hbm.1, f32[64,2,1024]{2,1,0:T(2,128)} %bitcast.3, bf16[2,1024,1024]{2,1,0:T(8,128)(2,1)} %d_hbm.1, bf16[2,1024,1024]{2,1,0:T(8,128)(2,1)} %c_hbm.1), custom_call_target="tpu_custom_call" | custom-call | tf_op jit(solution)/shard_map/pallas_call | solution.py:406
  73.4 1.9 %copy.6 = f32[1,64,2,1024]{3,2,1,0:T(2,128)} copy(f32[1,64,2,1024]{3,2,1,0:T(2,128)} %bitcast.2) | data formatting | bytes 1048576

commit v4 on v3

--- a/solution.py
+++ b/solution.py
@@ -10,6 +10,7 @@
 EDGE = 16
 DEG = 4
 STEPS = 2
+PARTS = 4
 GROUP = 4
 F32 = jnp.float32
 BF16 = jnp.bfloat16
@@ -82,6 +83,27 @@
     return jnp.concatenate([high, low, high], axis=0)
 
 
+def pack_symmetric(gram):
+    q = gram.shape[0] // 2
+    quarters = (gram[:q, :q], gram[q:, :q], gram[q:, q:])
+    cut = 3 * q // 4
+    tail = jnp.concatenate([block[cut:] for block in quarters], axis=0)
+    return jnp.concatenate([block[:cut] for block in quarters] + [tail], axis=1)
+
+
+def unpack_symmetric(packed, k):
+    q = k // 2
+    rest = q // 4
+    top, side, bottom = (
+        jnp.concatenate(
+            [packed[:, q * i : q * (i + 1)], packed[rest * i : rest * (i + 1), 3 * q :]], axis=0
+        )
+        for i in range(3)
+    )
+    upper = jnp.concatenate([top, jnp.transpose(side)], axis=1)
+    return jnp.concatenate([upper, jnp.concatenate([side, bottom], axis=1)], axis=0)
+
+
 def exact(a, b, dims):
     return lax.dot_general(
         a, b, dims, precision=lax.Precision.HIGHEST, preferred_element_type=F32
@@ -90,7 +112,7 @@
 
 def kernel(
     sizes, bounds_hbm, x_in, d_hbm, c_hbm, out,
-    bounds, x_own, dv, cv, ct, zf, zb, pb, rz, rp, acc, own, first, second, factors,
+    bounds, x_own, dv, cv, ct, zf, zb, pb, rz, rp, acc, own, first, second, factors, stack,
     ylow_out, ylow_in, high_out, high_in, corr_out, corr_in,
     load_sem, zs, zr, ps, pr, a1s, a1r, a2s, a2r, es, er, ready,
 ):
@@ -100,7 +122,7 @@
     cut = lax.axis_index("cuts")
     plane, member = me // GROUP, me % GROUP
     k, _, width = x_in.shape
-    half = width // 2
+    part = width // PARTS
     scale = 1.0 / (n_layer * 2 * width)
     has_prev, has_next = me > 0, me < n_layer - 1
     has_below, has_above = cut > 0, cut < n_cuts - 1
@@ -177,7 +199,7 @@
     def hear(r):
         pl.semaphore_wait(ready.at[r], 2)
 
-    columns = [pl.ds(h * half, half) for h in range(2)]
+    columns = [pl.ds(h * part, part) for h in range(PARTS)]
 
     def remote(src, dst, send, recv, device):
         return pltpu.make_async_remote_copy(
@@ -195,7 +217,7 @@
             pb.at[t, h], rp.at[t, h], ps.at[t, h], pr.at[t, h], {"layer": me + 1}
         )
 
-    lengths = [pl.ds(0, rows) for rows in (k // 2, k // 2, EDGE)]
+    lengths = [pl.ds(0, rows) for rows in (3 * k // 8, 3 * k // 8, EDGE)]
 
     def group_copy(i, q):
         return remote(
@@ -232,32 +254,30 @@
             total = total + second[i, q, lengths[i]]
         return total
 
-    def gram_start(i, src):
+    def gram_start(i, pairs):
         gram = jnp.zeros((2 * k, 2 * k), F32)
-        for l in range(2):
-            pair = jnp.concatenate(split(zf[src, l]), axis=0)
+        for pair in pairs:
             gram = gram + mm(pair, pair, NT)
-        gram = gram[:k, :k] + gram[:k, k:] + gram[k:, :k]
-        reduce_start(i, jnp.concatenate([gram[: k // 2], gram[k // 2 :]], axis=1))
+        reduce_start(i, pack_symmetric(gram[:k, :k] + gram[:k, k:] + gram[k:, :k]))
 
     def gram_end(i):
-        packed = reduce_end(i)
-        return jnp.concatenate([packed[:, :k], packed[:, k:]], axis=0) * scale
+        return unpack_symmetric(reduce_end(i), k) * scale
+
+    def first_gram():
+        gram_start(0, [jnp.concatenate(split(zf[0, l]), axis=0) for l in range(2)])
+
+    runs = STEPS * DEG
+
+    def send_product(t):
+        for h, s in enumerate(columns):
+            pb[t, h] = mm(zb[t, 1], cv[1, :, s]).astype(BF16)
+            pl.when(has_next)(lambda: p_copy(t, h).start())
 
     def apply_step(t, carry):
         cur, nxt = t % 2, (t + 1) % 2
         opening = t % DEG == 0
         factor, back = jnp.where(opening, 1.0, 2.0), jnp.where(opening, 0.0, 1.0)
-
-        @pl.when(has_prev)
-        def _():
-            z_copy(t, 0).start()
-            z_copy(t, 1).start()
-
-        @pl.when(t == 0)
-        def _():
-            tell(0)
-            loads[0].wait()
+        more = t + 1 < runs
 
         for r in range(rounds):
 
@@ -267,29 +287,15 @@
                 if r + 1 < rounds:
                     tell(r + 1)
 
-        for h, s in enumerate(columns):
-            pb[t, h] = mm(zb[t, 1], cv[1, :, s]).astype(BF16)
-
-            @pl.when(has_next)
-            def _():
-                p_copy(t, h).start()
-
-        @pl.when(t == 0)
-        def _():
-            for copy in loads[1:]:
-                copy.wait()
-            for l in (1, 0):
-                ct[l] = jnp.transpose(cv[l])
-
-        pl.when(t == DEG)(lambda: gram_start(0, 0))
+        pl.when(t == DEG)(first_gram)
         pl.when(t == DEG + 1)(lambda: reduce_middle(0))
 
         acc[0] = mm(zb[t, 0], dv[0]) + mm(zb[t, 1], ct[0])
         acc[1] = mm(zb[t, 1], dv[1]) + mm(zb[t, 0], cv[0])
 
-        @pl.when(t == 2 * DEG - 1)
+        @pl.when(t == runs - 1)
         def _():
-            factors[0] = stacked_factor(cholesky_inverse(gram_end(0)))
+            factors[...] = stacked_factor(cholesky_inverse(gram_end(0)))
 
         def update(l, s, total):
             now = zf[cur, l, :, s]
@@ -297,88 +303,95 @@
             zf[nxt, l, :, s] = value
             zb[t + 1, l, :, s] = value.astype(BF16)
 
-        pl.when(has_next)(lambda: z_copy(t, 0).wait_recv())
-        acc[1] += mm(rz[t, :, columns[0]], ct[1, columns[0], :])
-        pl.when(has_next)(lambda: z_copy(t, 1).wait_recv())
-        everything = pl.ds(0, width)
-        update(1, everything, acc[1] + mm(rz[t, :, columns[1]], ct[1, columns[1], :]))
+        for h, s in enumerate(columns):
+            pl.when(has_next)(lambda: z_copy(t, h).wait_recv())
+            total = acc[1] + mm(rz[t, :, s], ct[1, s, :])
+            if h + 1 < PARTS:
+                acc[1] = total
+            else:
+                update(1, pl.ds(0, width), total)
+
+        pl.when(more)(lambda: send_product(t + 1))
 
         for h, s in enumerate(columns):
             pl.when(has_prev)(lambda: p_copy(t, h).wait_recv())
             update(0, s, acc[0, :, s] + rp[t, h].astype(F32))
+            pl.when(jnp.logical_and(has_prev, more))(lambda: z_copy(t + 1, h).start())
         return carry
 
-    runs = STEPS * DEG
+    for h in range(PARTS):
+        pl.when(has_prev)(lambda: z_copy(0, h).start())
+    tell(0)
+    loads[0].wait()
+    send_product(0)
+    for copy in loads[1:]:
+        copy.wait()
+    for l in (1, 0):
+        ct[l] = jnp.transpose(cv[l])
     lax.fori_loop(0, runs, apply_step, 0)
-
-    for l in range(2):
-        value = mm(factors[0], stacked_rows(zf[0, l]))
-        zf[0, l] = value
-        ylow_out[l] = value[:EDGE].astype(BF16)
 
     below, above = {"cuts": cut - 1}, {"cuts": cut + 1}
     ylow_copy = remote(ylow_out, ylow_in, es.at[0], er.at[0], below)
-    high_copy = remote(high_out, high_in, es.at[1], er.at[1], above)
-    corr_copy = remote(corr_out, corr_in, es.at[2], er.at[2], above)
+    cross_copy = remote(corr_out, corr_in, es.at[1], er.at[1], above)
+    high_copies = [
+        remote(high_out.at[l], high_in.at[l], es.at[2 + l], er.at[2 + l], above) for l in range(2)
+    ]
+    for l in range(2):
+        stack[l] = stacked_rows(zf[0, l])
+        ylow_out[l] = mm(factors[:EDGE], stack[l]).astype(BF16)
     pl.when(has_below)(ylow_copy.start)
-    gram_start(1, 0)
+    for l in range(2):
+        stack[l] = stacked_rows(mm(factors[...], stack[l]))
+    gram_start(1, [stack[l, : 2 * k] for l in range(2)])
     reduce_middle(1)
 
     pl.when(has_above)(ylow_copy.wait_recv)
-    cross = jnp.zeros((k, EDGE), F32)
+    cross = jnp.zeros((EDGE, k), F32)
     corner = jnp.zeros((EDGE, EDGE), F32)
     for l in range(2):
-        y_high, y_low = split(zf[0, l])
-        cross = cross + mm(y_high, ylow_in[l], NT) + mm(y_low, ylow_in[l], NT)
+        cross = cross + mm(ylow_in[l], stack[l, :k], NT) + mm(ylow_in[l], stack[l, k : 2 * k], NT)
         corner = corner + mm(ylow_in[l], ylow_in[l], NT)
-    pieces = [cross[EDGE * i : EDGE * (i + 1)] for i in range(k // EDGE)] + [corner]
-    pieces.append(jnp.zeros((EDGE, 128 - EDGE * len(pieces)), F32))
-    packed = jnp.concatenate(pieces, axis=1)
-    reduce_start(2, packed)
+    blank = jnp.zeros((EDGE, 128 - k - EDGE), F32)
+    reduce_start(2, jnp.concatenate([cross, corner, blank], axis=1))
     reduce_middle(2)
 
     factor = cholesky_inverse(gram_end(1))
-    factors[0] = stacked_factor(factor)
     factor_edge = factor[k - EDGE :]
     edge_rows = stacked_factor(factor_edge)
     for l in range(2):
-        high_out[l] = mm(edge_rows, stacked_rows(zf[0, l])).astype(BF16)
-    pl.when(has_above)(high_copy.start)
-    for l in range(2):
-        zf[1, l] = mm(factors[0], stacked_rows(zf[0, l]))
+        high_out[l] = mm(edge_rows, stack[l]).astype(BF16)
+        pl.when(has_above)(high_copies[l].start)
+    all_rows = stacked_factor(factor)
+    for l in range(2):
+        zf[1, l] = mm(all_rows, stack[l])
         out[EDGE : k - EDGE, l, :] = zf[1, l, EDGE : k - EDGE]
 
     packed = reduce_end(2) * scale
-    cross = jnp.concatenate(
-        [packed[:, EDGE * i : EDGE * (i + 1)] for i in range(k // EDGE)], axis=0
-    )
+    projected = exact(packed[:, :k], factor_edge, NT)
+    corr_out[...] = jnp.concatenate([projected, jnp.zeros((EDGE, 128 - EDGE), F32)], axis=1)
+    pl.when(has_above)(cross_copy.start)
+
     corner = packed[:, k : k + EDGE]
     rows_at = lax.broadcasted_iota(jnp.int32, (EDGE, EDGE), 0)
     lanes_at = lax.broadcasted_iota(jnp.int32, (EDGE, EDGE), 1)
     corner = jnp.where(has_above, corner, (rows_at == lanes_at).astype(F32))
     above_factor = cholesky_inverse(corner)
-    corr = exact(exact(above_factor, cross, NT), factor_edge, NT)
-    corr_out[...] = jnp.concatenate([corr, jnp.zeros((EDGE, 128 - EDGE), F32)], axis=1)
-    pl.when(has_above)(corr_copy.start)
-
-    f_high, f_low = split(above_factor)
-    c_high, c_low = split(corr)
-    for l in range(2):
-        rows = mm(f_high, ylow_in[l]) + mm(f_low, ylow_in[l])
-        r_high, r_low = split(rows)
-        change = mm(c_high, r_high, TN) + mm(c_high, r_low, TN) + mm(c_low, r_high, TN)
+    corr = exact(above_factor, projected, NN)
+    w_high, w_low = split(exact(corr, above_factor, TN))
+    for l in range(2):
+        change = mm(w_high, ylow_in[l]) + mm(w_low, ylow_in[l])
         out[k - EDGE :, l, :] = zf[1, l, k - EDGE :] - change
 
-    pl.when(has_below)(high_copy.wait_recv)
-    pl.when(has_below)(corr_copy.wait_recv)
-    c_high, c_low = split(corr_in[:, :EDGE])
-    for l in range(2):
+    pl.when(has_below)(cross_copy.wait_recv)
+    c_high, c_low = split(exact(factor[:EDGE, :EDGE], corr_in[:, :EDGE], NN))
+    for l in range(2):
+        pl.when(has_below)(high_copies[l].wait_recv)
         change = mm(c_high, high_in[l]) + mm(c_low, high_in[l])
         out[:EDGE, l, :] = zf[1, l, :EDGE] - change
 
     pl.when(has_below)(ylow_copy.wait_send)
-    pl.when(has_above)(high_copy.wait_send)
-    pl.when(has_above)(corr_copy.wait_send)
+    for copy in [cross_copy] + high_copies:
+        pl.when(has_above)(copy.wait_send)
     for i in range(3):
         for q in range(GROUP - 1):
             group_copy(i, q).wait_send()
@@ -386,7 +399,7 @@
             plane_copy(i, q).wait_send()
 
     def drain(t, carry):
-        for h in range(2):
+        for h in range(PARTS):
             pl.when(has_prev)(lambda: z_copy(t, h).wait_send())
             pl.when(has_next)(lambda: p_copy(t, h).wait_send())
         return carry
@@ -416,14 +429,15 @@
             pltpu.VMEM((2, width, width), BF16),
             pltpu.VMEM((2, 2, k, width), F32),
             pltpu.VMEM((runs + 1, 2, k, width), BF16),
-            pltpu.VMEM((runs, 2, k, width // 2), BF16),
+            pltpu.VMEM((runs, PARTS, k, width // PARTS), BF16),
             pltpu.VMEM((runs, k, width), BF16),
-            pltpu.VMEM((runs, 2, k, width // 2), BF16),
+            pltpu.VMEM((runs, PARTS, k, width // PARTS), BF16),
             pltpu.VMEM((2, k, width), F32),
-            pltpu.VMEM((3, 2, k // 2, 128), F32),
-            pltpu.VMEM((3, GROUP - 1, k // 2, 128), F32),
-            pltpu.VMEM((3, n_z - 1, k // 2, 128), F32),
-            pltpu.VMEM((1, k, 3 * k), BF16),
+            pltpu.VMEM((3, 2, 3 * k // 8, 128), F32),
+            pltpu.VMEM((3, GROUP - 1, 3 * k // 8, 128), F32),
+            pltpu.VMEM((3, n_z - 1, 3 * k // 8, 128), F32),
+            pltpu.VMEM((k, 3 * k), BF16),
+            pltpu.VMEM((2, 3 * k, width), BF16),
             pltpu.VMEM((2, EDGE, width), BF16),
             pltpu.VMEM((2, EDGE, width), BF16),
             pltpu.VMEM((2, EDGE, width), BF16),
@@ -431,16 +445,16 @@
             pltpu.VMEM((EDGE, 128), F32),
             pltpu.VMEM((EDGE, 128), F32),
             dma((6,)),
-            dma((runs, 2)),
-            dma((runs, 2)),
-            dma((runs, 2)),
-            dma((runs, 2)),
+            dma((runs, PARTS)),
+            dma((runs, PARTS)),
+            dma((runs, PARTS)),
+            dma((runs, PARTS)),
             dma((3, GROUP - 1)),
             dma((3, GROUP - 1)),
             dma((3, n_z - 1)),
             dma((3, n_z - 1)),
-            dma((3,)),
-            dma((3,)),
+            dma((4,)),
+            dma((4,)),
             pltpu.SemaphoreType.REGULAR((rounds,)),
         ],
         compiler_params=pltpu.CompilerParams(

time: 75.4 us -> 71.9 us (0.954)
  Pallas kernels: 73.4 us -> 69.9 us
    pallas_call x1, Pallas kernels: 73.4 us -> 69.9 us  [per_device(): pl.pallas_call(functools.partial(kernel, sizes), out_shape=jax.ShapeDtype...]
where the time goes in v4:
time: 71.9 us; the launch traced here: 71.8 us
  Pallas kernels  69.9 us (97%)
  local copies, waits for them, and re-layouts  1.87 us (3%)
    pallas_call x1, Pallas kernels, per_device(): pl.pallas_call(functools.partial(kernel, sizes), out_shape=jax.ShapeDtype...  69.9 us
    unnamed x1, local copies, waits for them, and re-layouts  1.87 us

profile of v4, /device:TPU:6, one launch (start us, length us, event | category | flops | bytes accessed | tf_op | source)
XLA Modules:
  0.0 71.8 jit_solution(4388503494069934731)
XLA Ops:
  0.0 69.9 %shard_map.46 = f32[64,2,1024]{2,1,0:T(2,128)} custom-call(s32[1,2]{1,0:T(1,128)} %bounds_hbm.1, f32[64,2,1024]{2,1,0:T(2,128)} %bitcast.3, bf16[2,1024,1024]{2,1,0:T(8,128)(2,1)} %d_hbm.1, bf16[2,1024,1024]{2,1,0:T(8,128)(2,1)} %c_hbm.1), custom_call_target="tpu_custom_call" | custom-call | tf_op jit(solution)/shard_map/pallas_call | solution.py:419
  69.9 1.9 %copy.6 = f32[1,64,2,1024]{3,2,1,0:T(2,128)} copy(f32[1,64,2,1024]{3,2,1,0:T(2,128)} %bitcast.2) | data formatting | bytes 1048576

commit v5 on v4

--- a/solution.py
+++ b/solution.py
@@ -113,8 +113,8 @@
 def kernel(
     sizes, bounds_hbm, x_in, d_hbm, c_hbm, out,
     bounds, x_own, dv, cv, ct, zf, zb, pb, rz, rp, acc, own, first, second, factors, stack,
-    ylow_out, ylow_in, high_out, high_in, corr_out, corr_in,
-    load_sem, zs, zr, ps, pr, a1s, a1r, a2s, a2r, es, er, ready,
+    ylow_out, ylow_in, high_out, high_in, tail_out, tail_in, cross_in,
+    load_sem, zs, zr, ps, pr, a1s, a1r, a2s, a2r, es, er, xs, xr, ready,
 ):
     n_cuts, n_layer = sizes
     n_z = n_layer // GROUP
@@ -168,7 +168,8 @@
     @pl.when(jnp.logical_not(has_below))
     def _():
         high_in[...] = jnp.zeros_like(high_in)
-        corr_in[...] = jnp.zeros_like(corr_in)
+        tail_in[...] = jnp.zeros_like(tail_in)
+        cross_in[...] = jnp.zeros_like(cross_in)
 
     @pl.when(jnp.logical_not(has_above))
     def _():
@@ -332,7 +333,14 @@
 
     below, above = {"cuts": cut - 1}, {"cuts": cut + 1}
     ylow_copy = remote(ylow_out, ylow_in, es.at[0], er.at[0], below)
-    cross_copy = remote(corr_out, corr_in, es.at[1], er.at[1], above)
+    tail_copy = remote(tail_out, tail_in, es.at[1], er.at[1], above)
+    cross_copies = [
+        remote(
+            own.at[2, 1, lengths[2]], cross_in.at[q], xs.at[q], xr.at[q],
+            {"cuts": cut + 1, "layer": ((plane + q) % n_z) * GROUP + member},
+        )
+        for q in far_first + [0]
+    ]
     high_copies = [
         remote(high_out.at[l], high_in.at[l], es.at[2 + l], er.at[2 + l], above) for l in range(2)
     ]
@@ -355,9 +363,16 @@
     reduce_start(2, jnp.concatenate([cross, corner, blank], axis=1))
     reduce_middle(2)
 
+    @pl.when(has_above)
+    def _():
+        for copy in cross_copies:
+            copy.start()
+
     factor = cholesky_inverse(gram_end(1))
     factor_edge = factor[k - EDGE :]
     edge_rows = stacked_factor(factor_edge)
+    tail_out[...] = jnp.concatenate([factor_edge, jnp.zeros((EDGE, 128 - k), F32)], axis=1)
+    pl.when(has_above)(tail_copy.start)
     for l in range(2):
         high_out[l] = mm(edge_rows, stack[l]).astype(BF16)
         pl.when(has_above)(high_copies[l].start)
@@ -368,9 +383,6 @@
 
     packed = reduce_end(2) * scale
     projected = exact(packed[:, :k], factor_edge, NT)
-    corr_out[...] = jnp.concatenate([projected, jnp.zeros((EDGE, 128 - EDGE), F32)], axis=1)
-    pl.when(has_above)(cross_copy.start)
-
     corner = packed[:, k : k + EDGE]
     rows_at = lax.broadcasted_iota(jnp.int32, (EDGE, EDGE), 0)
     lanes_at = lax.broadcasted_iota(jnp.int32, (EDGE, EDGE), 1)
@@ -382,15 +394,24 @@
         change = mm(w_high, ylow_in[l]) + mm(w_low, ylow_in[l])
         out[k - EDGE :, l, :] = zf[1, l, k - EDGE :] - change
 
-    pl.when(has_below)(cross_copy.wait_recv)
-    c_high, c_low = split(exact(factor[:EDGE, :EDGE], corr_in[:, :EDGE], NN))
+    @pl.when(has_below)
+    def _():
+        tail_copy.wait_recv()
+        for copy in cross_copies:
+            copy.wait_recv()
+
+    cross = cross_in[0]
+    for q in range(1, n_z):
+        cross = cross + cross_in[q]
+    projected = exact(cross[:, :k] * scale, tail_in[:, :k], NT)
+    c_high, c_low = split(exact(factor[:EDGE, :EDGE], projected, NN))
     for l in range(2):
         pl.when(has_below)(high_copies[l].wait_recv)
         change = mm(c_high, high_in[l]) + mm(c_low, high_in[l])
         out[:EDGE, l, :] = zf[1, l, :EDGE] - change
 
     pl.when(has_below)(ylow_copy.wait_send)
-    for copy in [cross_copy] + high_copies:
+    for copy in [tail_copy] + high_copies + cross_copies:
         pl.when(has_above)(copy.wait_send)
     for i in range(3):
         for q in range(GROUP - 1):
@@ -444,6 +465,7 @@
             pltpu.VMEM((2, EDGE, width), BF16),
             pltpu.VMEM((EDGE, 128), F32),
             pltpu.VMEM((EDGE, 128), F32),
+            pltpu.VMEM((n_z, EDGE, 128), F32),
             dma((6,)),
             dma((runs, PARTS)),
             dma((runs, PARTS)),
@@ -455,12 +477,17 @@
             dma((3, n_z - 1)),
             dma((4,)),
             dma((4,)),
+            dma((n_z,)),
+            dma((n_z,)),
             pltpu.SemaphoreType.REGULAR((rounds,)),
         ],
         compiler_params=pltpu.CompilerParams(
-            collective_id=0, has_side_effects=True, vmem_limit_bytes=61 << 20
+            collective_id=0, has_side_effects=True, vmem_limit_bytes=48 << 20
         ),
-    )(bounds, x, diag_blocks, couplings)
+    )(*(
+        pltpu.with_memory_space_constraint(operand, pltpu.HBM)
+        for operand in (bounds, x, diag_blocks, couplings)
+    ))
     return result[None]
 
 

time: 71.9 us -> 68.3 us (0.950)
  Pallas kernels: 69.9 us -> 67.4 us
  local copies, waits for them, and re-layouts: 1.87 us -> 0.8 us
    pallas_call x1, Pallas kernels: 69.9 us -> 67.4 us  [per_device(): pl.pallas_call(functools.partial(kernel, sizes), out_shape=jax.ShapeDtype...]
    unnamed x1, local copies, waits for them, and re-layouts: 1.87 us -> 0.8 us
where the time goes in v5:
time: 68.3 us; the launch traced here: 68.2 us
  Pallas kernels  67.4 us (99%)
  local copies, waits for them, and re-layouts  0.8 us (1%)
    pallas_call x1, Pallas kernels, per_device(): pl.pallas_call(functools.partial(kernel, sizes), out_shape=jax.ShapeDtype...  67.4 us

profile of v5, /device:TPU:6, one launch (start us, length us, event | category | flops | bytes accessed | tf_op | source)
XLA Modules:
  0.0 68.2 jit_solution(833012145849831225)
XLA Ops:
  0.0 67.4 %shard_map.46 = f32[64,2,1024]{2,1,0:T(2,128)S(1)} custom-call(s32[1,2]{1,0:T(1,128)} %bounds_hbm.1, f32[64,2,1024]{2,1,0:T(2,128)} %bitcast.3, bf16[2,1024,1024]{2,1,0:T(8,128)(2,1)} %d_hbm.1, bf16[2,1024,1024]{2,1,0:T(8,128)(2,1)} %c_hbm.1), custom_call_target="tpu_custom_call" | custom-call | tf_op jit(solution)/shard_map/pallas_call | solution.py:440
  67.4 0.8 %copy.6 = f32[1,64,2,1024]{3,2,1,0:T(2,128)} copy(f32[1,64,2,1024]{3,2,1,0:T(2,128)S(1)} %bitcast.2) | data formatting | bytes 1048576

commit v6 on v5

--- a/solution.py
+++ b/solution.py
@@ -112,7 +112,7 @@
 
 def kernel(
     sizes, bounds_hbm, x_in, d_hbm, c_hbm, out,
-    bounds, x_own, dv, cv, ct, zf, zb, pb, rz, rp, acc, own, first, second, factors, stack,
+    bounds, x_own, dv, cv, ct, zf, zb, pb, rz, rp, acc, own, first, second, factors, stack, gram_part, gram_first,
     ylow_out, ylow_in, high_out, high_in, tail_out, tail_in, cross_in,
     load_sem, zs, zr, ps, pr, a1s, a1r, a2s, a2r, es, er, xs, xr, ready,
 ):
@@ -180,12 +180,13 @@
     high = bounds[0, 1].astype(F32) / 64.0
     centre = jnp.full((8, 128), (low + high) / 2.0, F32)[:1, :1]
     inverse = 1.0 / jnp.full((8, 128), (high - low) / 2.0, F32)[:1, :1]
-    x_load.wait()
-    for l in range(2):
+    def take(l):
         mine = x_own[:, l, :]
         zf[0, l] = mine
         zb[0, l] = mine.astype(BF16)
 
+    x_load.wait()
+    take(0)
     greeted = 2 + jnp.where(has_below, 1, 0) + jnp.where(has_above, 1, 0)
     pl.semaphore_wait(barrier, greeted)
 
@@ -255,17 +256,27 @@
             total = total + second[i, q, lengths[i]]
         return total
 
-    def gram_start(i, pairs):
-        gram = jnp.zeros((2 * k, 2 * k), F32)
-        for pair in pairs:
-            gram = gram + mm(pair, pair, NT)
+    def gram_start(i, grams):
+        gram = grams[0] + grams[1]
         reduce_start(i, pack_symmetric(gram[:k, :k] + gram[:k, k:] + gram[k:, :k]))
 
     def gram_end(i):
         return unpack_symmetric(reduce_end(i), k) * scale
 
     def first_gram():
-        gram_start(0, [jnp.concatenate(split(zf[0, l]), axis=0) for l in range(2)])
+        pairs = [jnp.concatenate(split(zf[0, l]), axis=0) for l in range(2)]
+        gram_start(0, [mm(pair, pair, NT) for pair in pairs])
+
+    core = member % 2
+
+    def close_low(l):
+        stack[l] = stacked_rows(zf[0, l])
+        ylow_out[l] = mm(factors[:EDGE], stack[l]).astype(BF16)
+
+    def close_rest(l):
+        stack[l] = stacked_rows(mm(factors[...], stack[l]))
+        pair = stack[l, : 2 * k]
+        return mm(pair, pair, NT)
 
     runs = STEPS * DEG
 
@@ -294,15 +305,36 @@
         acc[0] = mm(zb[t, 0], dv[0]) + mm(zb[t, 1], ct[0])
         acc[1] = mm(zb[t, 1], dv[1]) + mm(zb[t, 0], cv[0])
 
+        @pl.when(t == runs - 2)
+        def _():
+            gram_first[...] = gram_end(0)
+
         @pl.when(t == runs - 1)
         def _():
-            factors[...] = stacked_factor(cholesky_inverse(gram_end(0)))
+            factors[...] = stacked_factor(cholesky_inverse(gram_first[...]))
 
         def update(l, s, total):
             now = zf[cur, l, :, s]
             value = (factor * inverse) * (total - centre * now) - back * zf[nxt, l, :, s]
             zf[nxt, l, :, s] = value
             zb[t + 1, l, :, s] = value.astype(BF16)
+
+        def finish_first():
+            for h, s in enumerate(columns):
+                pl.when(has_prev)(lambda: p_copy(t, h).wait_recv())
+                update(0, s, acc[0, :, s] + rp[t, h].astype(F32))
+                pl.when(jnp.logical_and(has_prev, more))(lambda: z_copy(t + 1, h).start())
+
+        def close_early():
+            close_low(1 - core)
+            gram_part[...] = close_rest(1 - core)
+
+        early = jnp.logical_and(t == runs - 1, core == 1)
+
+        @pl.when(early)
+        def _():
+            finish_first()
+            close_early()
 
         for h, s in enumerate(columns):
             pl.when(has_next)(lambda: z_copy(t, h).wait_recv())
@@ -313,15 +345,13 @@
                 update(1, pl.ds(0, width), total)
 
         pl.when(more)(lambda: send_product(t + 1))
-
-        for h, s in enumerate(columns):
-            pl.when(has_prev)(lambda: p_copy(t, h).wait_recv())
-            update(0, s, acc[0, :, s] + rp[t, h].astype(F32))
-            pl.when(jnp.logical_and(has_prev, more))(lambda: z_copy(t + 1, h).start())
+        pl.when(jnp.logical_and(t == runs - 1, core == 0))(close_early)
+        pl.when(jnp.logical_not(early))(finish_first)
         return carry
 
     for h in range(PARTS):
         pl.when(has_prev)(lambda: z_copy(0, h).start())
+    take(1)
     tell(0)
     loads[0].wait()
     send_product(0)
@@ -344,13 +374,9 @@
     high_copies = [
         remote(high_out.at[l], high_in.at[l], es.at[2 + l], er.at[2 + l], above) for l in range(2)
     ]
-    for l in range(2):
-        stack[l] = stacked_rows(zf[0, l])
-        ylow_out[l] = mm(factors[:EDGE], stack[l]).astype(BF16)
+    close_low(core)
     pl.when(has_below)(ylow_copy.start)
-    for l in range(2):
-        stack[l] = stacked_rows(mm(factors[...], stack[l]))
-    gram_start(1, [stack[l, : 2 * k] for l in range(2)])
+    gram_start(1, [close_rest(core), gram_part[...]])
     reduce_middle(1)
 
     pl.when(has_above)(ylow_copy.wait_recv)
@@ -459,6 +485,8 @@
             pltpu.VMEM((3, n_z - 1, 3 * k // 8, 128), F32),
             pltpu.VMEM((k, 3 * k), BF16),
             pltpu.VMEM((2, 3 * k, width), BF16),
+            pltpu.VMEM((2 * k, 2 * k), F32),
+            pltpu.VMEM((k, k), F32),
             pltpu.VMEM((2, EDGE, width), BF16),
             pltpu.VMEM((2, EDGE, width), BF16),
             pltpu.VMEM((2, EDGE, width), BF16),

time: 68.3 us -> 69.5 us (1.018)
  Pallas kernels: 67.4 us -> 68.6 us
    pallas_call x1, Pallas kernels: 67.4 us -> 68.6 us  [per_device(): pl.pallas_call(functools.partial(kernel, sizes), out_shape=jax.ShapeDtype...]
where the time goes in v6:
time: 69.5 us; the launch traced here: 69.4 us
  Pallas kernels  68.6 us (99%)
  local copies, waits for them, and re-layouts  0.8 us (1%)
    pallas_call x1, Pallas kernels, per_device(): pl.pallas_call(functools.partial(kernel, sizes), out_shape=jax.ShapeDtype...  68.6 us

profile of v6, /device:TPU:6, one launch (start us, length us, event | category | flops | bytes accessed | tf_op | source)
XLA Modules:
  0.0 69.4 jit_solution(6920353645524115629)
XLA Ops:
  0.0 68.6 %shard_map.46 = f32[64,2,1024]{2,1,0:T(2,128)S(1)} custom-call(s32[1,2]{1,0:T(1,128)} %bounds_hbm.1, f32[64,2,1024]{2,1,0:T(2,128)} %bitcast.3, bf16[2,1024,1024]{2,1,0:T(8,128)(2,1)} %d_hbm.1, bf16[2,1024,1024]{2,1,0:T(8,128)(2,1)} %c_hbm.1), custom_call_target="tpu_custom_call" | custom-call | tf_op jit(solution)/shard_map/pallas_call | solution.py:466
  68.7 0.8 %copy.6 = f32[1,64,2,1024]{3,2,1,0:T(2,128)} copy(f32[1,64,2,1024]{3,2,1,0:T(2,128)S(1)} %bitcast.2) | data formatting | bytes 1048576

commit v7 on v5

--- a/solution.py
+++ b/solution.py
@@ -138,8 +138,7 @@
     for i, (src, dst) in enumerate(((c_hbm, cv), (d_hbm, dv))):
         for l in (1, 0):
             loads.append(pltpu.make_async_copy(src.at[l], dst.at[l], load_sem.at[2 * i + l]))
-    for copy in loads:
-        copy.start()
+    loads[0].start()
 
     barrier = pltpu.get_barrier_semaphore()
 
@@ -180,12 +179,13 @@
     high = bounds[0, 1].astype(F32) / 64.0
     centre = jnp.full((8, 128), (low + high) / 2.0, F32)[:1, :1]
     inverse = 1.0 / jnp.full((8, 128), (high - low) / 2.0, F32)[:1, :1]
-    x_load.wait()
-    for l in range(2):
+    def take(l):
         mine = x_own[:, l, :]
         zf[0, l] = mine
         zb[0, l] = mine.astype(BF16)
 
+    x_load.wait()
+    take(0)
     greeted = 2 + jnp.where(has_below, 1, 0) + jnp.where(has_above, 1, 0)
     pl.semaphore_wait(barrier, greeted)
 
@@ -289,10 +289,11 @@
                     tell(r + 1)
 
         pl.when(t == DEG)(first_gram)
-        pl.when(t == DEG + 1)(lambda: reduce_middle(0))
 
         acc[0] = mm(zb[t, 0], dv[0]) + mm(zb[t, 1], ct[0])
         acc[1] = mm(zb[t, 1], dv[1]) + mm(zb[t, 0], cv[0])
+
+        pl.when(t == DEG + 1)(lambda: reduce_middle(0))
 
         @pl.when(t == runs - 1)
         def _():
@@ -322,8 +323,11 @@
 
     for h in range(PARTS):
         pl.when(has_prev)(lambda: z_copy(0, h).start())
+    take(1)
     tell(0)
     loads[0].wait()
+    for copy in loads[1:]:
+        copy.start()
     send_product(0)
     for copy in loads[1:]:
         copy.wait()

time: 68.3 us -> 69.8 us (1.022)
  Pallas kernels: 67.4 us -> 68.7 us
    pallas_call x1, Pallas kernels: 67.4 us -> 68.7 us  [per_device(): pl.pallas_call(functools.partial(kernel, sizes), out_shape=jax.ShapeDtype...]
where the time goes in v7:
time: 69.8 us; the launch traced here: 69.5 us
  Pallas kernels  68.7 us (98%)
  local copies, waits for them, and re-layouts  0.8 us (1%)
    pallas_call x1, Pallas kernels, per_device(): pl.pallas_call(functools.partial(kernel, sizes), out_shape=jax.ShapeDtype...  68.7 us

profile of v7, /device:TPU:6, one launch (start us, length us, event | category | flops | bytes accessed | tf_op | source)
XLA Modules:
  0.0 69.5 jit_solution(16380502041439864339)
XLA Ops:
  0.0 68.7 %shard_map.46 = f32[64,2,1024]{2,1,0:T(2,128)S(1)} custom-call(s32[1,2]{1,0:T(1,128)} %bounds_hbm.1, f32[64,2,1024]{2,1,0:T(2,128)} %bitcast.3, bf16[2,1024,1024]{2,1,0:T(8,128)(2,1)} %d_hbm.1, bf16[2,1024,1024]{2,1,0:T(8,128)(2,1)} %c_hbm.1), custom_call_target="tpu_custom_call" | custom-call | tf_op jit(solution)/shard_map/pallas_call | solution.py:444
  68.7 0.8 %copy.6 = f32[1,64,2,1024]{3,2,1,0:T(2,128)} copy(f32[1,64,2,1024]{3,2,1,0:T(2,128)S(1)} %bitcast.2) | data formatting | bytes 1048576
